TPU v7x, 32 devices: a whole 2x2x4 slice. The times are simulated.
32 devices in a mesh: expert: 8 (over z, x), shard: 4 (over y, core).
Axes of the slice: x: 2, y: 2, z: 4, core: 2. Of those that a mesh axis runs over, the one named last changes fastest.
Arguments:
- tokens: bfloat16 [25216, 768], P(('expert', 'shard')), may hold values from -6 to 6
- routes: int32 [25216, 2], P(('expert', 'shard')), may hold values from 0 to 7, as said below
- capacity: int32 [8], replicated, may hold values from 100 to 200
- ln1_gain: float32 [768], replicated, may hold values from 0.5 to 1.5
- ln1_bias: float32 [768], replicated, may hold values from -1.5 to 1.5
- ln2_gain: float32 [768], replicated, may hold values from 0.5 to 1.5
- ln2_bias: float32 [768], replicated, may hold values from -1.5 to 1.5
- w_qkv: bfloat16 [768, 2304], P('shard'), may hold values from -0.21875 to 0.21875
- w_proj: bfloat16 [768, 768], P('shard'), may hold values from -0.875 to 0.875
- w_router: bfloat16 [768, 8], P('shard'), may hold values from -1 to 1
- w_in: bfloat16 [8, 768, 3072], P('expert'), may hold values from -0.21875 to 0.21875
- w_out: bfloat16 [8, 3072, 768], P('expert'), may hold values from -0.4375 to 0.4375
- cotangent: bfloat16 [25216, 768], P(('expert', 'shard')), may hold values from -6 to 6
Outputs:
- mixed: bfloat16 [25216, 768], P(('expert', 'shard'))
- balance_loss: float32 [], replicated
- grad_tokens: float32 [25216, 768], P(('expert', 'shard'))
- grad_ln1_gain: float32 [768], P('shard')
- grad_ln1_bias: float32 [768], P('shard')
- grad_ln2_gain: float32 [768], P('shard')
- grad_ln2_bias: float32 [768], P('shard')
- grad_qkv_weight: float32 [768, 2304], P('shard')
- grad_proj: float32 [768, 768], P('shard')
- grad_router: float32 [768, 8], P('shard')
- grad_expert_in: float32 [8, 768, 3072], P('expert', None, 'shard')
- grad_expert_out: float32 [8, 3072, 768], P('expert', 'shard')
Inputs may be any that keep to these rules, and one draw needn't show every extreme that they name: `routes`: each row names two different experts.
All inputs are finite; a program needn't handle non-finite values.
Results may differ from a plain program's by a relative error of at most 0.012.
Values may be sent and summed in bfloat16 or wider, within the bound.
No kernel may reach another device: no remote copies, remote signals or barrier semaphores. Data moves between devices by JAX's collectives and lax.ppermute only.
A program may use at most 192 MiB of HBM per device.

v0:
```python
import math

import jax
import jax.numpy as jnp
from jax import lax
from jax.sharding import PartitionSpec as P

HEADS = 12
SEQ = 197


NORM_EPS = 1e-06
LOSS_WEIGHT = 0.01


def norm_rows(values, norm_gain, norm_bias):
    row_mean = jnp.mean(values, axis=-1, keepdims=True)
    centered = values - row_mean
    variance = jnp.mean(centered * centered, axis=-1, keepdims=True)
    inverse = lax.rsqrt(variance + NORM_EPS)
    normed = centered * inverse
    return (normed * norm_gain + norm_bias, normed, inverse)


def norm_back(grad_rows, normed, inverse, norm_gain):
    scaled = grad_rows * norm_gain
    inner_term = (
        scaled
        - jnp.mean(scaled, axis=-1, keepdims=True)
        - normed * jnp.mean(scaled * normed, axis=-1, keepdims=True)
    )
    return (inverse * inner_term, jnp.sum(grad_rows * normed, axis=0), jnp.sum(grad_rows, axis=0))


def gelu_slope(pre_act):
    normal_cdf = 0.5 * (1.0 + lax.erf(pre_act * (1.0 / math.sqrt(2.0))))
    density = jnp.exp(-0.5 * pre_act * pre_act) * (1.0 / math.sqrt(2.0 * math.pi))
    return normal_cdf + pre_act * density


def times_transposed(left, right):
    return lax.dot_general(
        left, right, (((1,), (1,)), ((), ())), preferred_element_type=jnp.float32
    )


def over_rows(left, right):
    return lax.dot_general(
        left, right, (((0,), (0,)), ((), ())), preferred_element_type=jnp.float32
    )


def route_slots(route_rows, capacity, expert_count):
    labels = jnp.arange(expert_count, dtype=jnp.int32)
    first_hit = (route_rows[:, 0:1] == labels[None, :]).astype(jnp.int32)
    second_hit = (route_rows[:, 1:2] == labels[None, :]).astype(jnp.int32)
    before_first = jnp.cumsum(first_hit, axis=0) - first_hit
    before_second = (
        jnp.cumsum(second_hit, axis=0) - second_hit + jnp.sum(first_hit, axis=0, keepdims=True)
    )
    slot_first = jnp.sum(before_first * first_hit, axis=1)
    slot_second = jnp.sum(before_second * second_hit, axis=1)
    limit_first = jnp.sum(first_hit * capacity[None, :], axis=1)
    limit_second = jnp.sum(second_hit * capacity[None, :], axis=1)
    slot_index = jnp.stack([slot_first, slot_second], axis=1)
    kept_mask = slot_index < jnp.stack([limit_first, limit_second], axis=1)
    return (slot_index, kept_mask, first_hit + second_hit)


def body(
    tokens,
    routes,
    capacity,
    ln1_gain,
    ln1_bias,
    ln2_gain,
    ln2_bias,
    w_qkv,
    w_proj,
    w_router,
    w_in,
    w_out,
    cotangent,
):
    row_count, model_width = tokens.shape
    expert_count = capacity.shape[0]
    local_experts = w_in.shape[0]
    owners = lax.axis_size("expert")
    shards = lax.axis_size("shard")
    seq_len = SEQ
    head_count = HEADS
    head_dim = model_width // head_count
    images = row_count // seq_len
    slot_count = 8 * ((2 * row_count + 8 * expert_count - 1) // (8 * expert_count))
    buffer_rows = expert_count * slot_count
    all_tokens = row_count * owners * shards
    score_scale = 1.0 / math.sqrt(head_dim)
    token_rows = tokens.astype(jnp.float32)
    qkv_full, proj_full, router_full = (
        lax.all_gather(w_qkv, "shard", axis=0, tiled=True),
        lax.all_gather(w_proj, "shard", axis=0, tiled=True),
        lax.all_gather(w_router, "shard", axis=0, tiled=True),
    )
    first_normed, normed_one, inverse_one = norm_rows(token_rows, ln1_gain, ln1_bias)
    first_low = first_normed.astype(jnp.bfloat16)
    qkv_rows = jnp.dot(first_low, qkv_full, preferred_element_type=jnp.float32).astype(jnp.bfloat16)
    qkv_parts = qkv_rows.reshape(images, seq_len, 3, head_count, head_dim)
    query_rows = qkv_parts[:, :, 0]
    key_rows = qkv_parts[:, :, 1]
    value_rows = qkv_parts[:, :, 2]
    scores = (
        jnp.einsum("bqhd,bkhd->bhqk", query_rows, key_rows, preferred_element_type=jnp.float32)
        * score_scale
    )
    score_peak = jnp.max(scores, axis=-1, keepdims=True)
    exp_scores = jnp.exp(scores - score_peak)
    exp_total = jnp.sum(exp_scores, axis=-1, keepdims=True)
    log_total = score_peak + jnp.log(exp_total)
    attention = (exp_scores / exp_total).astype(jnp.bfloat16)
    heads_mixed = jnp.einsum(
        "bhqk,bkhd->bqhd", attention, value_rows, preferred_element_type=jnp.float32
    )
    heads_out = heads_mixed.reshape(row_count, model_width).astype(jnp.bfloat16)
    after_attention = token_rows + jnp.dot(heads_out, proj_full, preferred_element_type=jnp.float32)
    mid_normed, normed_two, inverse_two = norm_rows(after_attention, ln2_gain, ln2_bias)
    mid_low = mid_normed.astype(jnp.bfloat16)
    logits = jnp.dot(mid_low, router_full, preferred_element_type=jnp.float32)
    gate_probs = jax.nn.softmax(logits, axis=-1)
    slot_index, kept_mask, route_hits = route_slots(routes, capacity, expert_count)
    counts = jnp.sum(route_hits, axis=0).astype(jnp.float32)
    prob_sum = jnp.sum(gate_probs, axis=0)
    count_all, prob_all = lax.psum((counts, prob_sum), ("expert", "shard"))
    route_share = count_all / (2.0 * all_tokens)
    balance_loss = expert_count * jnp.sum(route_share * prob_all / all_tokens)
    target = jnp.where(kept_mask, routes * slot_count + slot_index, buffer_rows)
    flat_target = target.reshape(-1)
    safe_target = jnp.minimum(target, buffer_rows - 1)
    gates = jnp.take_along_axis(gate_probs, routes, axis=1)
    pair_weight = jnp.where(kept_mask, gates, 0.0)
    pair_rows = jnp.broadcast_to(mid_low[:, None, :], (row_count, 2, model_width)).reshape(
        -1, model_width
    )
    send_rows = (
        jnp.zeros((buffer_rows, model_width), jnp.bfloat16)
        .at[flat_target]
        .set(pair_rows, mode="drop")
    )
    send_rows = send_rows.reshape(owners, local_experts, slot_count, model_width)
    arrived = lax.all_to_all(send_rows, "expert", split_axis=0, concat_axis=0, tiled=True)
    pre_act = jnp.einsum("sjcd,jdf->sjcf", arrived, w_in, preferred_element_type=jnp.float32)
    hidden = jax.nn.gelu(pre_act, approximate=False).astype(jnp.bfloat16)
    expert_made = jnp.einsum(
        "sjcf,jfd->sjcd", hidden, w_out, preferred_element_type=jnp.float32
    ).astype(jnp.bfloat16)
    returned = lax.all_to_all(
        expert_made, "expert", split_axis=0, concat_axis=0, tiled=True
    ).reshape(buffer_rows, model_width)
    picked = jnp.take(returned, safe_target, axis=0).astype(jnp.float32)
    layer_out = after_attention + jnp.sum(picked * pair_weight[..., None], axis=1)
    mixed = layer_out.astype(jnp.bfloat16)
    grad_out = cotangent.astype(jnp.float32)
    grad_gate = jnp.where(kept_mask, jnp.sum(picked * grad_out[:, None, :], axis=-1), 0.0)
    grad_pair = (
        (pair_weight[..., None] * grad_out[:, None, :])
        .astype(jnp.bfloat16)
        .reshape(-1, model_width)
    )
    grad_send = (
        jnp.zeros((buffer_rows, model_width), jnp.bfloat16)
        .at[flat_target]
        .set(grad_pair, mode="drop")
    )
    grad_send = grad_send.reshape(owners, local_experts, slot_count, model_width)
    grad_made = lax.all_to_all(grad_send, "expert", split_axis=0, concat_axis=0, tiled=True)
    grad_hidden = jnp.einsum("sjcd,jfd->sjcf", grad_made, w_out, preferred_element_type=jnp.float32)
    grad_pre = (grad_hidden * gelu_slope(pre_act)).astype(jnp.bfloat16)
    grad_arrived = jnp.einsum(
        "sjcf,jdf->sjcd", grad_pre, w_in, preferred_element_type=jnp.float32
    ).astype(jnp.bfloat16)
    grad_back = lax.all_to_all(
        grad_arrived, "expert", split_axis=0, concat_axis=0, tiled=True
    ).reshape(buffer_rows, model_width)
    grad_in_whole = jnp.einsum(
        "sjcd,sjcf->jdf", arrived, grad_pre, preferred_element_type=jnp.float32
    )
    grad_out_whole = jnp.einsum(
        "sjcf,sjcd->jfd", hidden, grad_made, preferred_element_type=jnp.float32
    )
    grad_expert_in, grad_expert_out = (
        lax.psum_scatter(grad_in_whole, "shard", scatter_dimension=2, tiled=True),
        lax.psum_scatter(grad_out_whole, "shard", scatter_dimension=1, tiled=True),
    )
    qkv_back, proj_back, router_back = (
        lax.all_gather(w_qkv, "shard", axis=0, tiled=True),
        lax.all_gather(w_proj, "shard", axis=0, tiled=True),
        lax.all_gather(w_router, "shard", axis=0, tiled=True),
    )
    labels = jnp.arange(expert_count, dtype=jnp.int32)
    route_onehot = (routes[:, :, None] == labels[None, None, :]).astype(jnp.float32)
    grad_probs = LOSS_WEIGHT * expert_count * route_share[None, :] / all_tokens + jnp.sum(
        route_onehot * grad_gate[..., None], axis=1
    )
    grad_logits = (
        gate_probs * (grad_probs - jnp.sum(gate_probs * grad_probs, axis=-1, keepdims=True))
    ).astype(jnp.bfloat16)
    grad_router = over_rows(mid_low, grad_logits)
    taken = jnp.take(grad_back, safe_target, axis=0).astype(jnp.float32)
    grad_mid = jnp.sum(jnp.where(kept_mask[..., None], taken, 0.0), axis=1) + times_transposed(
        grad_logits, router_back
    )
    grad_mid_in, grad_gain_two, grad_bias_two = norm_back(
        grad_mid, normed_two, inverse_two, ln2_gain
    )
    grad_after = grad_out + grad_mid_in
    grad_heads = grad_after.astype(jnp.bfloat16)
    grad_proj = over_rows(heads_out, grad_heads)
    grad_heads_out = (
        times_transposed(grad_heads, proj_back)
        .astype(jnp.bfloat16)
        .reshape(images, seq_len, head_count, head_dim)
    )
    scores_again = (
        jnp.einsum("bqhd,bkhd->bhqk", query_rows, key_rows, preferred_element_type=jnp.float32)
        * score_scale
    )
    probs_again = jnp.exp(scores_again - log_total)
    grad_attention = jnp.einsum(
        "bqhd,bkhd->bhqk", grad_heads_out, value_rows, preferred_element_type=jnp.float32
    )
    inner_sum = jnp.sum(probs_again * grad_attention, axis=-1, keepdims=True)
    grad_scores = (probs_again * (grad_attention - inner_sum)).astype(jnp.bfloat16)
    grad_values = jnp.einsum(
        "bhqk,bqhd->bkhd",
        probs_again.astype(jnp.bfloat16),
        grad_heads_out,
        preferred_element_type=jnp.float32,
    )
    grad_queries = (
        jnp.einsum("bhqk,bkhd->bqhd", grad_scores, key_rows, preferred_element_type=jnp.float32)
        * score_scale
    )
    grad_keys = (
        jnp.einsum("bhqk,bqhd->bkhd", grad_scores, query_rows, preferred_element_type=jnp.float32)
        * score_scale
    )
    grad_qkv = (
        jnp.stack([grad_queries, grad_keys, grad_values], axis=2)
        .reshape(row_count, 3 * model_width)
        .astype(jnp.bfloat16)
    )
    grad_qkv_weight = over_rows(first_low, grad_qkv)
    grad_first = times_transposed(grad_qkv, qkv_back)
    grad_first_in, grad_gain_one, grad_bias_one = norm_back(
        grad_first, normed_one, inverse_one, ln1_gain
    )
    grad_tokens = grad_after + grad_first_in
    shares = (
        lax.psum_scatter(grad_qkv_weight, "shard", scatter_dimension=0, tiled=True),
        lax.psum_scatter(grad_proj, "shard", scatter_dimension=0, tiled=True),
        lax.psum_scatter(grad_router, "shard", scatter_dimension=0, tiled=True),
        lax.psum_scatter(grad_gain_one, "shard", scatter_dimension=0, tiled=True),
        lax.psum_scatter(grad_bias_one, "shard", scatter_dimension=0, tiled=True),
        lax.psum_scatter(grad_gain_two, "shard", scatter_dimension=0, tiled=True),
        lax.psum_scatter(grad_bias_two, "shard", scatter_dimension=0, tiled=True),
    )
    totals = lax.psum(
        (shares[0], shares[1], shares[2], shares[3], shares[4], shares[5], shares[6]), "expert"
    )
    return (
        mixed,
        balance_loss,
        grad_tokens,
        totals[3],
        totals[4],
        totals[5],
        totals[6],
        totals[0],
        totals[1],
        totals[2],
        grad_expert_in,
        grad_expert_out,
    )


def solution(mesh):
    in_specs = (
        P(("expert", "shard"), None),
        P(("expert", "shard"), None),
        P(),
        P(),
        P(),
        P(),
        P(),
        P("shard", None),
        P("shard", None),
        P("shard", None),
        P("expert", None, None),
        P("expert", None, None),
        P(("expert", "shard"), None),
    )
    out_specs = (
        P(("expert", "shard"), None),
        P(),
        P(("expert", "shard"), None),
        P("shard"),
        P("shard"),
        P("shard"),
        P("shard"),
        P("shard", None),
        P("shard", None),
        P("shard", None),
        P("expert", None, "shard"),
        P("expert", "shard", None),
    )
    return jax.shard_map(body, mesh=mesh, in_specs=in_specs, out_specs=out_specs, check_vma=False)
```

profile of v0, /device:TPU:0, one launch (start us, length us, event | category | flops | bytes accessed | tf_op | source)
XLA Modules:
  0.0 943.7 jit_solution(842858472382141031)
XLA Ops:
  13.6 6.4 all-gather
  20.5 2.0 reduce-window.14
  23.0 2.0 reduce-window.16
  28.6 14.5 %all-gather.4.cloned.1.call-done = bf16[768,2304]{1,0:T(8,128)(2,1)} async-done(((bf16[192,2304]{1,0:T(8,128)(2,1)}), bf16[768,2304]{1,0:T(8,128)(2,1)}) %all-gather.4.cloned.1.call-update) | async-done | bytes 3538960 | tf_op jit(solution)/shard_map/all_gather | solution.py:100
  43.1 6.9 convolution_convert_fusion
  50.0 11.9 %reshape.378 = bf16[4,197,3,12,64]{4,3,2,1,0:T(8,128)(2,1)} reshape(bf16[788,2304]{1,0:T(8,128)(2,1)} %convolution_convert_fusion) | data formatting | bytes 7262208 | tf_op jit(solution)/shard_map/reshape | solution.py:107
  61.9 6.9 fusion.186
  68.9 3.9 copy.236
  72.8 4.5 copy.237
  78.8 2.2 fusion.31
  81.0 2.2 copy-done
  83.3 3.4 copy.235
  86.7 6.6 fusion.96
  94.5 2.1 convert_element_type.107
  96.6 3.0 fusion.187
  102.4 15.3 %gather_fusion = f32[1576]{0:T(1024)S(1)} fusion(f32[788,8]{0,1:T(8,128)S(1)} %fusion.117, s32[1576]{0:T(1024)S(1)} %reshape.327), kind=kCustom, calls=%fused_computation.2 | custom fusion | bytes 25216 | tf_op jit(solution)/shard_map/jit(take_along_axis)/gather | solution.py:138
  119.4 2.6 broadcast_in_dim.30
  122.1 6.2 reshape.337
  128.3 13.0 %scatter_custom_fusion = bf16[1600,768]{1,0:T(8,128)(2,1)} fusion(s32[1576]{0:T(1024)S(1)} %fusion.120, bf16[1576,768]{1,0:T(8,128)(2,1)} %reshape.337, bf16[]{:T(256)} %constant.31.clone.1), kind=kCustom, calls=%fused_computation.129 | custom fusion | bytes 2458112 | tf_op jit(solution)/shard_map/scatter | solution.py:146
  141.3 5.5 all-to-all-start
  146.9 3.5 mul.251
  150.3 7.1 mul.252
  157.8 19.1 %scatter_custom_fusion.1 = bf16[1600,768]{1,0:T(8,128)(2,1)} fusion(s32[1576]{0:T(1024)S(1)} %fusion.120, f32[1576,768]{1,0:T(8,128)} %mul.252, f32[1576]{0:T(1024)S(1)} %mul.249, bf16[]{:T(256)} %constant.31.clone.1), kind=kCustom, calls=%fused_computation.107 | custom fusion | flops 2420736 | bytes 7307266 | tf_op jit(solution)/shard_map/scatter | solution.py:171
  177.0 26.4 %all-to-all-done = bf16[8,1,200,768]{3,2,1,0:T(8,128)(2,1)} async-done(((bf16[8,1,200,768]{3,2,1,0:T(8,128)(2,1)}), bf16[8,1,200,768]{3,2,1,0:T(8,128)(2,1)}, u32[]{:S(2)}, u32[]{:S(2)}) %all-to-all-start) | async-done | bytes 2457632 | tf_op jit(solution)/shard_map/all_to_all | solution.py:149
  203.4 4.1 all-to-all-start.2
  207.5 14.2 %fusion.49 = f32[8,200,3072]{2,1,0:T(8,128)} fusion(bf16[1,768,3072]{2,1,0:T(8,128)(2,1)} %param.25, bf16[8,1,200,768]{3,2,1,0:T(8,128)(2,1)} %all-to-all-done), kind=kOutput, calls=%fused_computation.74 | convolution fusion | flops 7549747200 | bytes 26836992 | tf_op jit(solution)/shard_map/sjcd,jdf->sjcf/dot_general | solution.py:150
  221.7 41.9 %all-to-all-done.2 = bf16[8,1,200,768]{3,2,1,0:T(8,128)(2,1)S(1)} async-done(((bf16[8,1,200,768]{3,2,1,0:T(8,128)(2,1)}), bf16[8,1,200,768]{3,2,1,0:T(8,128)(2,1)S(1)}, u32[]{:S(2)}, u32[]{:S(2)}) %all-to-all-start.2) | async-done | bytes 2457632 | tf_op jit(solution)/shard_map/all_to_all | solution.py:174
  263.5 17.2 %fusion.8 = bf16[8,1,200,3072]{3,2,0,1:T(8,128)(2,1)S(1)} fusion(f32[8,200,3072]{2,1,0:T(8,128)} %fusion.49, bf16[1,3072,768]{2,1,0:T(8,128)(2,1)} %param.26, bf16[8,1,200,768]{3,2,1,0:T(8,128)(2,1)S(1)} %all-to-all-done.2), kind=kOutput, calls=%fused_computation.15 | convolution fusion | flops 7598899200 | bytes 36667392 | tf_op jit(solution)/shard_map/sjcd,jfd->sjcf/dot_general | solution.py:175
  280.8 3.7 copy-done.73
  284.5 11.4 %convert_bitcast_fusion = bf16[8,1,200,768]{3,2,1,0:T(8,128)(2,1)} fusion(bf16[1,768,3072]{2,1,0:T(8,128)(2,1)} %param.25, bf16[8,1,200,3072]{3,2,0,1:T(8,128)(2,1)S(1)} %fusion.8), kind=kOutput, calls=%fused_computation.91 | convolution fusion | flops 7550976000 | bytes 17006592 | tf_op jit(solution)/shard_map/sjcf,jdf->sjcd/dot_general | solution.py:177
  296.0 3.8 all-to-all-start.3
  299.8 53.0 %convert_bitcast_fusion.1 = bf16[8,1,200,768]{3,2,1,0:T(8,128)(2,1)} fusion(bf16[1,3072,768]{2,1,0:T(8,128)(2,1)} %param.26, f32[8,200,3072]{2,1,0:T(8,128)} %fusion.49), kind=kOutput, calls=%fused_computation.92 | convolution fusion | flops 7870464000 | bytes 26836992 | tf_op jit(solution)/shard_map/sjcf,jfd->sjcd/dot_general | solution.py:152
  352.8 3.1 all-to-all-done.3
  355.9 4.4 all-to-all-start.1
  360.4 75.5 %psum.63 = f32[8]{0:T(128)S(1)} all-reduce(f32[8]{0:T(128)S(1)} %convert_element_type.118), channel_id=1, replica_groups=mesh['expert'=8,'shard'=4] {'expert','shard'}, use_global_device_ids=true, to_apply=%region_20.22 | all-reduce | flops 8 | bytes 64 | tf_op jit(solution)/shard_map/psum | solution.py:132
  435.9 2.9 convert_element_type.119
  439.7 6.2 gather_fusion.2
  445.9 6.1 reshape.367
  452.0 9.4 gather_fusion.1
  461.4 2.3 reshape.363
  463.8 23.6 %fusion.45 = (f32[788,2]{1,0:T(8,128)S(1)}, f32[788,768]{1,0:T(8,128)}, f32[788,768]{1,0:T(8,128)}) fusion(f32[788,768]{1,0:T(8,128)} %convert_element_type.119, bf16[788,2,768]{2,1,0:T(2,128)(2,1)} %reshape.363, pred[788,2]{1,0:T(8,128)(4,1)S(1)} %copy.204, f32[788,2]{1,0:T(8,128)S(1)} %copy-done.21, bf16[788,2,768]{2,1,0:T(2,128)(2,1)} %reshape.367, ...), kind=kLoop, calls=%fused_computation.65 | loop fusion | flops 10891736 | bytes 12119440 | tf_op jit(solution)/shard_map/reduce_sum | solution.py:162
  488.4 3.8 multiply_reduce_fusion.2
  492.2 2.1 multiply_add_fusion
  495.7 2.8 fusion.108
  499.1 2.9 convolution_convert_fusion.1
  502.0 3.6 reshape.379
  505.5 4.1 copy.219
  509.6 7.6 multiply_reduce_fusion
  517.3 11.7 %multiply_convert_fusion = bf16[4,12,197,197]{2,3,1,0:T(8,128)(2,1)} fusion(f32[4,12,197,197]{2,3,1,0:T(8,128)} %get-tuple-element.62, f32[4,12,197,197]{2,3,1,0:T(8,128)} %copy-done, f32[4,12,197]{2,1,0:T(8,128)S(1)} %get-tuple-element.61, f32[4,12,197]{2,1,0:T(8,128)S(1)} %log_add_fusion), kind=kLoop, calls=%fused_computation.47 | loop fusion | flops 9314160 | bytes 18703968 | tf_op jit(solution)/shard_map/convert_element_type | solution.py:231
  528.9 3.6 fusion.99
  535.0 5.7 fusion.93
  542.0 6.6 copy.224
  548.7 9.7 %convert_element_type.132 = bf16[788,2304]{0,1:T(8,128)(2,1)} reshape(bf16[4,197,3,12,64]{1,0,4,3,2:T(4,128)(2,1)} %copy.224) | data formatting | bytes 7262208 | tf_op jit(solution)/shard_map/convert_element_type | solution.py:249
  558.4 8.6 fusion.183
  569.7 51.8 %fusion.36 = f32[1,3072,768]{2,1,0:T(8,128)} fusion(f32[8,200,3072]{2,1,0:T(8,128)} %fusion.49, bf16[8,1,200,768]{3,2,1,0:T(8,128)(2,1)} %copy-done.22), kind=kOutput, calls=%fused_computation.58 | convolution fusion | flops 7869235200 | bytes 31555584 | tf_op jit(solution)/shard_map/sjcf,sjcd->jfd/dot_general | solution.py:186
  621.6 14.4 %fusion.33 = f32[1,768,3072]{2,1,0:T(8,128)} fusion(bf16[8,1,200,3072]{3,2,0,1:T(8,128)(2,1)} %copy-done.73, bf16[8,1,200,768]{3,2,1,0:T(8,128)(2,1)} %all-to-all-done), kind=kOutput, calls=%fused_computation.57 | convolution fusion | flops 7549747200 | bytes 21725184 | tf_op jit(solution)/shard_map/sjcd,sjcf->jdf/dot_general | solution.py:183
  638.1 38.8 %psum.64 = f32[8]{0:T(128)S(1)} all-reduce(f32[8]{0:T(128)S(1)} %copy-done.65), channel_id=1, replica_groups=mesh['expert'=8,'shard'=4] {'expert','shard'}, use_global_device_ids=true, to_apply=%region_22.24 | all-reduce | flops 8 | bytes 64 | tf_op jit(solution)/shard_map/psum | solution.py:132
  677.0 8.7 fusion.69
  685.6 11.5 %all-reduce.8 = (f32[768]{0:T(1024)S(1)}, f32[768]{0:T(1024)S(1)}, f32[768]{0:T(1024)S(1)}, f32[768]{0:T(1024)S(1)}) all-reduce(f32[768]{0:T(1024)S(1)} %get-tuple-element.15, f32[768]{0:T(1024)S(1)} %get-tuple-element.22, f32[768]{0:T(1024)S(1)} %copy-done.55, ...), channel_id=2, replica_groups=mesh['expert'=8,'shard'=4] {'shard'}, use_global_device_ids=true, to_apply=%region_35.37.clone | all-reduce | flops 3072 | bytes 24576
  698.7 3.9 fusion.68
  703.6 36.6 %all-reduce.6 = (f32[192]{0:T(256)}, f32[192]{0:T(256)}, f32[192]{0:T(256)}, f32[192]{0:T(256)}, f32[192,8]{0,1:T(8,128)}) all-reduce(f32[192]{0:T(256)S(1)} %dynamic-slice.1, f32[192]{0:T(256)S(1)} %dynamic-slice.3, f32[192]{0:T(256)S(1)} %dynamic-slice.5, ...), channel_id=1, replica_groups=mesh['expert'=8,'shard'=4] {'expert'}, use_global_device_ids=true, to_apply=%region_36.38 | all-reduce | flops 2304 | bytes 18432 | tf_op jit(solution)/shard_map/psum | solution.py:266
  740.2 77.6 %reduce-scatter.12.cloned.1.call-done = f32[1,768,768]{2,1,0:T(8,128)} async-done(((f32[1,768,3072]{2,1,0:T(8,128)}), f32[1,768,768]{2,1,0:T(8,128)}) %reduce-scatter.12.cloned.1.call-update) | async-done | bytes 2359312 | tf_op jit(solution)/shard_map/reduce_scatter | solution.py:190
  817.8 112.7 %all-reduce.11.cloned.1.call-done = (f32[192,2304]{1,0:T(8,128)}, f32[192,768]{1,0:T(8,128)}) async-done(((f32[192,2304]{1,0:T(8,128)}, f32[192,768]{1,0:T(8,128)}), (f32[192,2304]{1,0:T(8,128)}, f32[192,768]{1,0:T(8,128)})) %all-reduce.11.cloned.1.call-update) | async-done | bytes 2359312 | tf_op jit(solution)/shard_map/psum | solution.py:266
  930.6 2.8 copy.240
  (243 shorter events, 34.0 us)
Async XLA Ops:
  7.2 35.9 %copy-start.11 = (bf16[788,768]{1,0:T(8,128)(2,1)S(1)}, bf16[788,768]{1,0:T(8,128)(2,1)}, u32[]{:S(2)}) copy-start(bf16[788,768]{1,0:T(8,128)(2,1)} %param.15) | copy-start | bytes 3631108
  7.2 18.4 %copy-start.64 = (s32[8]{0:T(128)S(1)}, s32[8]{0:T(128)}, u32[]{:S(2)}) copy-start(s32[8]{0:T(128)} %param.17) | copy-start | bytes 100
  7.2 35.9 %copy-start.60 = (f32[768]{0:T(1024)S(1)}, f32[768]{0:T(1024)}, u32[]{:S(2)}) copy-start(f32[768]{0:T(1024)} %param.18) | copy-start | bytes 9220
  7.2 35.9 %copy-start.68 = (f32[768]{0:T(1024)S(1)}, f32[768]{0:T(1024)}, u32[]{:S(2)}) copy-start(f32[768]{0:T(1024)} %param.19) | copy-start | bytes 9220
  7.2 35.9 %all-gather.4.cloned.1.call-start = ((), (), s32[]{:S(2)}) async-start(), calls=%async_computation.9 | async-start | bytes 4423680 | tf_op jit(solution)/shard_map/all_gather | solution.py:100
  8.0 88.6 %all-gather.6.cloned.1.call-start = ((), (), s32[]{:S(2)}) async-start(), calls=%async_computation.10 | async-start | bytes 1474560 | tf_op jit(solution)/shard_map/all_gather | solution.py:101
  11.8 38.3 %copy-start.46 = (f32[788]{0:T(1024)}, f32[788]{0:T(1024)S(1)}, u32[]{:S(2)}) copy-start(f32[788]{0:T(1024)S(1)} %broadcast_multiply_fusion.5) | copy-start | bytes 9460
  13.6 36.4 %copy-start.52 = (f32[788]{0:T(1024)}, f32[788]{0:T(1024)S(1)}, u32[]{:S(2)}) copy-start(f32[788]{0:T(1024)S(1)} %add_rsqrt_fusion.1) | copy-start | bytes 9460
  20.0 80.6 %copy-start.32 = (bf16[768,8]{0,1:T(8,128)(2,1)}, bf16[768,8]{0,1:T(8,128)(2,1)S(1)}, u32[]{:S(2)}) copy-start(bf16[768,8]{0,1:T(8,128)(2,1)S(1)} %reshape.359) | copy-start | bytes 36868
  72.8 6.0 copy-start.6
  78.8 4.4 copy-start
  78.8 7.8 copy-start.26
  78.8 4.4 copy-start.10
  83.3 10.0 %copy-start.28 = (f32[4,12,197]{2,1,0:T(8,128)}, f32[4,12,197]{2,1,0:T(8,128)S(1)}, u32[]{:S(2)}) copy-start(f32[4,12,197]{2,1,0:T(8,128)S(1)} %fusion.31) | copy-start | bytes 113476
  100.6 18.8 %copy-start.4 = (bf16[788,768]{1,0:T(8,128)(2,1)}, bf16[788,768]{1,0:T(8,128)(2,1)S(1)}, u32[]{:S(2)}) copy-start(bf16[788,768]{1,0:T(8,128)(2,1)S(1)} %add_convert_fusion.1) | copy-start | bytes 3631108
  102.3 15.9 %copy-start.30 = (s32[788,2]{0,1:T(2,128)S(1)}, s32[788,2]{0,1:T(2,128)}, u32[]{:S(2)}) copy-start(s32[788,2]{0,1:T(2,128)} %param.16) | copy-start | bytes 18916
  102.3 15.9 %copy-start.49 = (s32[788,1]{0,1:T(1,128)S(1)}, s32[788,1]{0,1:T(1,128)}, u32[]{:S(2)}) copy-start(s32[788,1]{0,1:T(1,128)} %stack.35) | copy-start | bytes 9460
  102.3 15.9 %copy-start.50 = (s32[788,1]{0,1:T(1,128)S(1)}, s32[788,1]{0,1:T(1,128)}, u32[]{:S(2)}) copy-start(s32[788,1]{0,1:T(1,128)} %stack.34) | copy-start | bytes 9460
  102.3 15.9 %copy-start.57 = (s32[788,1]{0,1:T(1,128)S(1)}, s32[788,1]{0,1:T(1,128)}, u32[]{:S(2)}) copy-start(s32[788,1]{0,1:T(1,128)} %stack.37) | copy-start | bytes 9460
  102.3 15.9 %copy-start.58 = (s32[788,1]{0,1:T(1,128)S(1)}, s32[788,1]{0,1:T(1,128)}, u32[]{:S(2)}) copy-start(s32[788,1]{0,1:T(1,128)} %stack.38) | copy-start | bytes 9460
  128.3 18.6 %copy-start.15 = (bf16[788,768]{1,0:T(8,128)(2,1)S(1)}, bf16[788,768]{1,0:T(8,128)(2,1)}, u32[]{:S(2)}) copy-start(bf16[788,768]{1,0:T(8,128)(2,1)} %param.27) | copy-start | bytes 3631108
  141.3 62.0 %all-to-all-start = ((bf16[8,1,200,768]{3,2,1,0:T(8,128)(2,1)}), bf16[8,1,200,768]{3,2,1,0:T(8,128)(2,1)}, u32[]{:S(2)}, u32[]{:S(2)}) async-start(bf16[8,1,200,768]{3,2,1,0:T(8,128)(2,1)} %bitcast.212), calls=%async_computation | async-start | bytes 4915200 | tf_op jit(solution)/shard_map/all_to_all | solution.py:149
  157.6 45.8 %copy-start.20 = (f32[788,2]{1,0:T(8,128)}, f32[788,2]{1,0:T(8,128)S(1)}, u32[]{:S(2)}) copy-start(f32[788,2]{1,0:T(8,128)S(1)} %copy.211) | copy-start | bytes 18916
  203.4 60.2 %all-to-all-start.2 = ((bf16[8,1,200,768]{3,2,1,0:T(8,128)(2,1)}), bf16[8,1,200,768]{3,2,1,0:T(8,128)(2,1)S(1)}, u32[]{:S(2)}, u32[]{:S(2)}) async-start(bf16[8,1,200,768]{3,2,1,0:T(8,128)(2,1)} %bitcast.31), calls=%async_computation.2 | async-start | bytes 4915200 | tf_op jit(solution)/shard_map/all_to_all | solution.py:174
  263.5 17.2 %copy-start.22 = (bf16[8,1,200,768]{3,2,1,0:T(8,128)(2,1)}, bf16[8,1,200,768]{3,2,1,0:T(8,128)(2,1)S(1)}, u32[]{:S(2)}) copy-start(bf16[8,1,200,768]{3,2,1,0:T(8,128)(2,1)S(1)} %all-to-all-done.2) | copy-start | bytes 7372804
  296.0 60.0 %all-to-all-start.3 = ((bf16[8,1,200,768]{3,2,1,0:T(8,128)(2,1)}), bf16[8,1,200,768]{3,2,1,0:T(8,128)(2,1)S(1)}, u32[]{:S(2)}, u32[]{:S(2)}) async-start(bf16[8,1,200,768]{3,2,1,0:T(8,128)(2,1)} %convert_bitcast_fusion), calls=%async_computation.3 | async-start | bytes 4915200 | tf_op jit(solution)/shard_map/all_to_all | solution.py:180
  352.8 7.6 copy-start.66
  352.8 85.9 %copy-start.43 = (pred[788,2]{0,1:T(4,128)(4,1)S(1)}, pred[788,2]{0,1:T(4,128)(4,1)}, u32[]{:S(2)}) copy-start(pred[788,2]{0,1:T(4,128)(4,1)} %copy-done.42) | copy-start | bytes 4732
  352.8 86.2 %copy-start.51 = (s32[788,2]{0,1:T(2,128)S(1)}, s32[788,2]{0,1:T(2,128)}, u32[]{:S(2)}) copy-start(s32[788,2]{0,1:T(2,128)} %get-tuple-element.47) | copy-start | bytes 18916
  352.8 86.6 %copy-start.59 = (pred[788,2]{0,1:T(4,128)(4,1)S(1)}, pred[788,2]{0,1:T(4,128)(4,1)}, u32[]{:S(2)}) copy-start(pred[788,2]{0,1:T(4,128)(4,1)} %get-tuple-element.46) | copy-start | bytes 4732
  355.9 96.1 %all-to-all-start.1 = ((bf16[8,1,200,768]{3,2,1,0:T(8,128)(2,1)}), bf16[8,1,200,768]{3,2,1,0:T(8,128)(2,1)}, u32[]{:S(2)}, u32[]{:S(2)}) async-start(bf16[8,1,200,768]{3,2,1,0:T(8,128)(2,1)} %convert_bitcast_fusion.1), calls=%async_computation.1 | async-start | bytes 4915200 | tf_op jit(solution)/shard_map/all_to_all | solution.py:155
  360.3 275.9 %reduce-scatter.10.cloned.1.call-start = ((), (), s32[]{:S(2)}) async-start(), calls=%async_computation.12 | async-start | bytes 2949120 | tf_op jit(solution)/shard_map/reduce_scatter | solution.py:259
  435.9 10.1 %copy-start.71 = (f32[8]{0:T(128)}, f32[8]{0:T(128)S(1)}, u32[]{:S(2)}) copy-start(f32[8]{0:T(128)S(1)} %psum.63) | copy-start | bytes 100
  463.7 23.8 %copy-start.31 = (s32[788,2]{0,1:T(2,128)S(1)}, s32[788,2]{0,1:T(2,128)}, u32[]{:S(2)}) copy-start(s32[788,2]{0,1:T(2,128)} %param.16) | copy-start | bytes 18916
  463.7 23.9 %copy-start.25 = (f32[788,8]{0,1:T(8,128)S(1)}, f32[788,8]{0,1:T(8,128)}, u32[]{:S(2)}) copy-start(f32[788,8]{0,1:T(8,128)} %copy-done.24) | copy-start | bytes 75652
  463.7 23.9 %copy-start.37 = (f32[788]{0:T(1024)S(1)}, f32[788]{0:T(1024)}, u32[]{:S(2)}) copy-start(f32[788]{0:T(1024)} %copy-done.36) | copy-start | bytes 9460
  463.7 23.9 %copy-start.41 = (f32[788]{0:T(1024)S(1)}, f32[788]{0:T(1024)}, u32[]{:S(2)}) copy-start(f32[788]{0:T(1024)} %copy-done.40) | copy-start | bytes 9460
  463.7 24.6 %copy-start.3 = (f32[788,768]{1,0:T(8,128)S(1)}, f32[788,768]{1,0:T(8,128)}, u32[]{:S(2)}) copy-start(f32[788,768]{1,0:T(8,128)} %copy-done.2) | copy-start | bytes 7262212
  463.8 24.6 %copy-start.33 = (bf16[768,8]{0,1:T(8,128)(2,1)S(1)}, bf16[768,8]{0,1:T(8,128)(2,1)}, u32[]{:S(2)}) copy-start(bf16[768,8]{0,1:T(8,128)(2,1)} %copy-done.32) | copy-start | bytes 36868
  463.8 24.6 %copy-start.35 = (f32[788]{0:T(1024)S(1)}, f32[788]{0:T(1024)}, u32[]{:S(2)}) copy-start(f32[788]{0:T(1024)} %copy-done.34) | copy-start | bytes 9460
  463.8 24.6 %copy-start.39 = (f32[788]{0:T(1024)S(1)}, f32[788]{0:T(1024)}, u32[]{:S(2)}) copy-start(f32[788]{0:T(1024)} %copy-done.38) | copy-start | bytes 9460
  463.8 24.6 %copy-start.45 = (f32[768]{0:T(1024)S(1)}, f32[768]{0:T(1024)}, u32[]{:S(2)}) copy-start(f32[768]{0:T(1024)} %param.20) | copy-start | bytes 9220
  487.5 4.7 copy-start.16
  487.5 4.7 copy-start.17
  498.6 137.6 %reduce-scatter.8.cloned.1.call-start = ((), (), s32[]{:S(2)}) async-start(), calls=%async_computation.11 | async-start | bytes 8847360 | tf_op jit(solution)/shard_map/reduce_scatter | solution.py:258
  502.0 7.7 copy-start.19
  517.3 11.7 %copy-start.9 = (bf16[4,197,1,12,64]{1,4,3,0,2:T(8,128)(2,1)S(1)}, bf16[4,197,1,12,64]{1,4,3,0,2:T(8,128)(2,1)}, u32[]{:S(2)}) copy-start(bf16[4,197,1,12,64]{1,4,3,0,2:T(8,128)(2,1)} %copy-done.8) | copy-start | bytes 3631108
  528.9 4.4 copy-start.7
  548.7 9.7 %copy-start.13 = (bf16[788,768]{1,0:T(8,128)(2,1)S(1)}, bf16[788,768]{1,0:T(8,128)(2,1)}, u32[]{:S(2)}) copy-start(bf16[788,768]{1,0:T(8,128)(2,1)} %param.15) | copy-start | bytes 3631108
  548.7 9.7 %copy-start.47 = (f32[788]{0:T(1024)S(1)}, f32[788]{0:T(1024)}, u32[]{:S(2)}) copy-start(f32[788]{0:T(1024)} %copy-done.46) | copy-start | bytes 9460
  548.7 9.7 %copy-start.53 = (f32[788]{0:T(1024)S(1)}, f32[788]{0:T(1024)}, u32[]{:S(2)}) copy-start(f32[788]{0:T(1024)} %copy-done.52) | copy-start | bytes 9460
  548.7 9.7 %copy-start.61 = (f32[768]{0:T(1024)S(1)}, f32[768]{0:T(1024)}, u32[]{:S(2)}) copy-start(f32[768]{0:T(1024)} %param.18) | copy-start | bytes 9220
  548.7 9.7 %copy-start.69 = (f32[768]{0:T(1024)S(1)}, f32[768]{0:T(1024)}, u32[]{:S(2)}) copy-start(f32[768]{0:T(1024)} %param.19) | copy-start | bytes 9220
  567.1 135.6 %reduce-scatter.16.cloned.1.call-start = ((), (), s32[]{:S(2)}) async-start(), calls=%async_computation.15 | async-start | bytes 491520
  569.7 170.5 %reduce-scatter.14.cloned.1.call-start = ((), (), s32[]{:S(2)}) async-start(), calls=%async_computation.14 | async-start | bytes 11796480 | tf_op jit(solution)/shard_map/reduce_scatter | solution.py:191
  621.6 196.3 %reduce-scatter.12.cloned.1.call-start = ((), (), s32[]{:S(2)}) async-start(), calls=%async_computation.13 | async-start | bytes 11796480 | tf_op jit(solution)/shard_map/reduce_scatter | solution.py:190
  636.0 40.9 %copy-start.14 = (bf16[788,768]{1,0:T(8,128)(2,1)S(1)}, bf16[788,768]{1,0:T(8,128)(2,1)}, u32[]{:S(2)}) copy-start(bf16[788,768]{1,0:T(8,128)(2,1)} %param.15) | copy-start | bytes 3631108
  636.0 40.9 %copy-start.48 = (f32[788]{0:T(1024)S(1)}, f32[788]{0:T(1024)}, u32[]{:S(2)}) copy-start(f32[788]{0:T(1024)} %copy-done.46) | copy-start | bytes 9460
  636.1 40.9 %copy-start.54 = (f32[788]{0:T(1024)S(1)}, f32[788]{0:T(1024)}, u32[]{:S(2)}) copy-start(f32[788]{0:T(1024)} %copy-done.52) | copy-start | bytes 9460
  636.1 40.9 %copy-start.62 = (f32[768]{0:T(1024)S(1)}, f32[768]{0:T(1024)}, u32[]{:S(2)}) copy-start(f32[768]{0:T(1024)} %param.18) | copy-start | bytes 9220
  636.1 294.5 %all-reduce.11.cloned.1.call-start = ((), (), s32[]{:S(2)}) async-start(), calls=%async_computation.16 | async-start | bytes 4718592 | tf_op jit(solution)/shard_map/psum | solution.py:266
  676.9 8.7 copy-start.55
  676.9 8.7 copy-start.56
  677.0 20.5 %copy-start.72 = (f32[8]{0:T(128)S(1)}, f32[8]{0:T(128)}, u32[]{:S(2)}) copy-start(f32[8]{0:T(128)} %copy-done.71) | copy-start | bytes 100
  (22 other events, 47.5 us)
Sparse Core Ops, SparseCore 0:
  9.6 33.4 all-gather.3
  44.7 17.4 all-gather.5
  498.7 32.9 reduce-scatter.9
  567.2 63.3 reduce-scatter.7
  633.5 20.9 reduce-scatter.15
  657.5 78.6 reduce-scatter.13
  739.3 78.4 reduce-scatter.11
  821.4 109.0 all-reduce.10
where the time goes:
time: 954 us; the launch traced here: 944 us
  waiting for transfers between devices  278 us (29%)
  matrix products  227 us (24%)
  blocking collectives  169 us (18%)
  local copies, waits for them, and re-layouts  154 us (16%)
  other arithmetic  79 us (8%)
  starting transfers between devices  18.6 us (2%)
  between operations  18.1 us (2%)
    psum x2, blocking collectives, body(): count_all, prob_all = lax.psum((counts, prob_sum), ('expert', 'shard'))  114 us
    psum x1, waiting for transfers between devices, body(): lax.psum((shares[0], shares[1], shares[2], shares[3], shares[4], shares[5...  113 us
    reduce_scatter x1, waiting for transfers between devices, body(): lax.psum_scatter(grad_in_whole, 'shard', scatter_dimension=2, tiled=True)  77.6 us
    dot_general x1, matrix products, body(): jnp.einsum('sjcf,jfd->sjcd', hidden, w_out, preferred_element_type=jnp.fl...  53 us
    dot_general x1, matrix products, body(): jnp.einsum('sjcf,sjcd->jfd', hidden, grad_made, preferred_element_type=jn...  51.8 us
    all_to_all x1, waiting for transfers between devices, body(): lax.all_to_all(grad_send, 'expert', split_axis=0, concat_axis=0, tiled=True)  41.9 us
    psum x1, blocking collectives, body(): lax.psum((shares[0], shares[1], shares[2], shares[3], shares[4], shares[5...  36.6 us
    unnamed x160, local copies, waits for them, and re-layouts  29.3 us
  transfers between devices with their start and end apart: 12, of which 6 were waited for; matrix products, arithmetic and copies ran while one was open for 35% of the time, Pallas kernels for 0%

commit v1 on v0

v1 whole, which is shorter than its diff:
```python
import functools
import math

import jax
import jax.numpy as jnp
from jax import lax
from jax.experimental import pallas as pl
from jax.experimental.pallas import tpu as pltpu
from jax.sharding import PartitionSpec as P

HEADS = 12
SEQ = 197
PAD_SEQ = 208
LANES = 128

NORM_EPS = 1e-06
LOSS_WEIGHT = 0.01
NEG = -1e30
VMEM_LIMIT = 56 * 1024 * 1024
BF = jnp.bfloat16
F32 = jnp.float32


def dot_nn(left, right):
    return lax.dot_general(left, right, (((1,), (0,)), ((), ())), preferred_element_type=F32)


def dot_nt(left, right):
    return lax.dot_general(left, right, (((1,), (1,)), ((), ())), preferred_element_type=F32)


def dot_tn(left, right):
    return lax.dot_general(left, right, (((0,), (0,)), ((), ())), preferred_element_type=F32)


def norm_rows(values):
    row_mean = jnp.mean(values, axis=-1, keepdims=True)
    centered = values - row_mean
    variance = jnp.mean(centered * centered, axis=-1, keepdims=True)
    inverse = lax.rsqrt(variance + NORM_EPS)
    return centered * inverse, inverse


def norm_back(grad_rows, normed, inverse, norm_gain):
    scaled = grad_rows * norm_gain
    return inverse * (
        scaled
        - jnp.mean(scaled, axis=-1, keepdims=True)
        - normed * jnp.mean(scaled * normed, axis=-1, keepdims=True)
    )


def attend_kernel(tok_ref, gain_ref, bias_ref, w_ref, first_ref, qkv_ref, heads_ref):
    width = tok_ref.shape[1]
    normed, _ = norm_rows(tok_ref[...].astype(F32))
    first = (normed * gain_ref[...] + bias_ref[...]).astype(BF)
    first_ref[...] = first
    for part in range(3):
        cols = slice(part * width, (part + 1) * width)
        qkv_ref[:, cols] = dot_nn(first, w_ref[:, cols]).astype(BF)
    rows = tok_ref.shape[0]
    lane = lax.broadcasted_iota(jnp.int32, (rows, LANES), 1)
    key_at = lax.broadcasted_iota(jnp.int32, (rows, rows), 1)
    scale = 1.0 / math.sqrt(width // HEADS)
    for pair in range(width // LANES):
        queries = qkv_ref[:, pair * LANES : (pair + 1) * LANES]
        keys = qkv_ref[:, width + pair * LANES : width + (pair + 1) * LANES]
        values = qkv_ref[:, 2 * width + pair * LANES : 2 * width + (pair + 1) * LANES]
        mixed = None
        for half in range(2):
            mine = (lane < LANES // 2) if half == 0 else (lane >= LANES // 2)
            zero = jnp.zeros_like(queries)
            scores = dot_nt(jnp.where(mine, queries, zero), keys) * scale
            scores = jnp.where(key_at < SEQ, scores, NEG)
            peak = jnp.max(scores, axis=-1, keepdims=True)
            weights = jnp.exp(scores - peak)
            total = jnp.sum(weights, axis=-1, keepdims=True)
            weights = (weights / total).astype(BF)
            term = dot_nn(weights, jnp.where(mine, values, zero))
            mixed = term if mixed is None else mixed + term
        heads_ref[:, pair * LANES : (pair + 1) * LANES] = mixed.astype(BF)


def attend(tok_pad, gain, bias, w_qkv, images):
    rows, width = tok_pad.shape
    whole = lambda i: (0, 0)
    block = lambda i: (i, 0)
    return pl.pallas_call(
        attend_kernel,
        grid=(images,),
        in_specs=[
            pl.BlockSpec((PAD_SEQ, width), block),
            pl.BlockSpec((1, width), whole),
            pl.BlockSpec((1, width), whole),
            pl.BlockSpec((width, 3 * width), whole),
        ],
        out_specs=[
            pl.BlockSpec((PAD_SEQ, width), block),
            pl.BlockSpec((PAD_SEQ, 3 * width), block),
            pl.BlockSpec((PAD_SEQ, width), block),
        ],
        out_shape=[
            jax.ShapeDtypeStruct((rows, width), BF),
            jax.ShapeDtypeStruct((rows, 3 * width), BF),
            jax.ShapeDtypeStruct((rows, width), BF),
        ],
        compiler_params=pltpu.CompilerParams(vmem_limit_bytes=VMEM_LIMIT),
        cost_estimate=pl.CostEstimate(
            flops=2 * rows * width * 3 * width + 4 * rows * PAD_SEQ * width,
            bytes_accessed=2 * (6 * rows * width + 3 * width * width),
            transcendentals=rows * PAD_SEQ * HEADS,
        ),
    )(tok_pad, gain.reshape(1, -1), bias.reshape(1, -1), w_qkv)


def attend_back_kernel(q_ref, k_ref, v_ref, g_ref, dq_ref, dk_ref, dv_ref, *, scale):
    rows, cols = q_ref.shape
    lane = lax.broadcasted_iota(jnp.int32, (rows, LANES), 1)
    key_at = lax.broadcasted_iota(jnp.int32, (rows, rows), 0)
    for pair in range(cols // LANES):
        at = slice(pair * LANES, (pair + 1) * LANES)
        queries, keys, values, grads = q_ref[:, at], k_ref[:, at], v_ref[:, at], g_ref[:, at]
        zero = jnp.zeros_like(queries)
        sums = None
        for half in range(2):
            mine = (lane < LANES // 2) if half == 0 else (lane >= LANES // 2)
            q_half = jnp.where(mine, queries, zero)
            g_half = jnp.where(mine, grads, zero)
            scores = dot_nt(keys, q_half) * scale
            scores = jnp.where(key_at < SEQ, scores, NEG)
            peak = jnp.max(scores, axis=0, keepdims=True)
            weights = jnp.exp(scores - peak)
            probs = weights / jnp.sum(weights, axis=0, keepdims=True)
            grad_attention = dot_nt(values, g_half)
            inner = jnp.sum(probs * grad_attention, axis=0, keepdims=True)
            grad_scores = (probs * (grad_attention - inner)).astype(BF)
            terms = (
                dot_tn(grad_scores, jnp.where(mine, keys, zero)),
                dot_nn(grad_scores, q_half),
                dot_nn(probs.astype(BF), g_half),
            )
            sums = terms if sums is None else tuple(a + b for a, b in zip(sums, terms))
        dq_ref[:, at] = (sums[0] * scale).astype(BF)
        dk_ref[:, at] = (sums[1] * scale).astype(BF)
        dv_ref[:, at] = sums[2].astype(BF)


def attend_back(qkv, grad_heads_out, images, group, groups):
    rows, width = grad_heads_out.shape
    cols = width // groups

    def at(part):
        return pl.BlockSpec((PAD_SEQ, cols), lambda i: (i, part * groups + group))

    out = pl.BlockSpec((PAD_SEQ, cols), lambda i: (i, 0))
    return pl.pallas_call(
        functools.partial(attend_back_kernel, scale=1.0 / math.sqrt(width // HEADS)),
        grid=(images,),
        in_specs=[at(0), at(1), at(2), at(0)],
        out_specs=[out] * 3,
        out_shape=[jax.ShapeDtypeStruct((rows, cols), BF)] * 3,
        compiler_params=pltpu.CompilerParams(vmem_limit_bytes=VMEM_LIMIT),
        cost_estimate=pl.CostEstimate(
            flops=10 * rows * PAD_SEQ * cols,
            bytes_accessed=2 * 7 * rows * cols,
            transcendentals=rows * PAD_SEQ * HEADS // groups,
        ),
    )(qkv, qkv, qkv, grad_heads_out)


def expert_kernel(
    me_ref, x_ref, c_ref, wr_ref, win_ref, wout_ref,
    hid_ref, gp_ref, gm_ref, mg_ref, rows_ref, gr_ref,
    made_ref, acc_ref, p_ref,
    *, experts, block,
):
    step = pl.program_id(0)
    last = pl.num_programs(0) - 1
    count = x_ref.shape[0] // block
    lane = lax.broadcasted_iota(jnp.int32, (block, LANES), 1)
    mine = lane == me_ref[0]

    @pl.when(step == 0)
    def _():
        for b in range(count):
            at = slice(b * block, (b + 1) * block)
            logits = jnp.where(lane < experts, dot_nn(x_ref[at, :], wr_ref[...]), NEG)
            top = jnp.max(logits, axis=-1, keepdims=True)
            weights = jnp.exp(logits - top)
            probs = weights / jnp.sum(weights, axis=-1, keepdims=True)
            p_ref[at, :] = probs
            gate = jnp.sum(jnp.where(mine, probs, 0.0), axis=-1, keepdims=True)
            gm_ref[at, :] = (gate * c_ref[at, :].astype(F32)).astype(BF)

    for b in range(count):
        at = slice(b * block, (b + 1) * block)
        pre = dot_nn(x_ref[at, :], win_ref[...])
        back = dot_nt(gm_ref[at, :], wout_ref[...])
        cdf = 0.5 * (1.0 + lax.erf(pre * (1.0 / math.sqrt(2.0))))
        density = jnp.exp(-0.5 * pre * pre) * (1.0 / math.sqrt(2.0 * math.pi))
        hidden = (pre * cdf).astype(BF)
        grad_pre = (back * (cdf + pre * density)).astype(BF)
        hid_ref[at, :] = hidden
        gp_ref[at, :] = grad_pre
        made = dot_nn(hidden, wout_ref[...])
        rows = dot_nt(grad_pre, win_ref[...])

        @pl.when(step == 0)
        def _():
            made_ref[at, :] = made
            acc_ref[at, :] = rows

        @pl.when(step > 0)
        def _():
            made_ref[at, :] += made
            acc_ref[at, :] += rows

    @pl.when(step == last)
    def _():
        total = None
        for b in range(count):
            at = slice(b * block, (b + 1) * block)
            probs = p_ref[at, :]
            gate = jnp.sum(jnp.where(mine, probs, 0.0), axis=-1, keepdims=True)
            made = made_ref[at, :]
            mg_ref[at, :] = (gate * made).astype(BF)
            gain = jnp.sum(c_ref[at, :].astype(F32) * made.astype(BF).astype(F32), axis=-1, keepdims=True)
            routed = (gain * gate * (jnp.where(mine, 1.0, 0.0) - probs)).astype(BF)
            rows_ref[at, :] = (acc_ref[at, :] + dot_nt(routed, wr_ref[...])).astype(BF)
            part = dot_tn(routed, x_ref[at, :])
            total = part if total is None else total + part
        gr_ref[...] = total


def run_expert(me, x, c, w_router, w_in, w_out, experts):
    rows, width = x.shape
    hidden = w_in.shape[1]
    tile = 256
    block = rows // 4
    whole = lambda j: (0, 0)
    col = lambda j: (0, j)
    row = lambda j: (j, 0)
    big = jax.ShapeDtypeStruct((rows, hidden), BF)
    small = jax.ShapeDtypeStruct((rows, width), BF)
    return pl.pallas_call(
        functools.partial(expert_kernel, experts=experts, block=block),
        grid=(hidden // tile,),
        in_specs=[
            pl.BlockSpec(memory_space=pltpu.SMEM),
            pl.BlockSpec((rows, width), whole),
            pl.BlockSpec((rows, width), whole),
            pl.BlockSpec((width, LANES), whole),
            pl.BlockSpec((width, tile), col),
            pl.BlockSpec((tile, width), row),
        ],
        out_specs=[
            pl.BlockSpec((rows, tile), col),
            pl.BlockSpec((rows, tile), col),
            pl.BlockSpec((rows, width), whole),
            pl.BlockSpec((rows, width), whole),
            pl.BlockSpec((rows, width), whole),
            pl.BlockSpec((LANES, width), whole),
        ],
        out_shape=[big, big, small, small, small, jax.ShapeDtypeStruct((LANES, width), F32)],
        scratch_shapes=[
            pltpu.VMEM((rows, width), F32),
            pltpu.VMEM((rows, width), F32),
            pltpu.VMEM((rows, LANES), F32),
        ],
        compiler_params=pltpu.CompilerParams(vmem_limit_bytes=VMEM_LIMIT),
        cost_estimate=pl.CostEstimate(
            flops=8 * rows * width * hidden,
            bytes_accessed=4 * (rows * hidden + width * hidden + 3 * rows * width),
            transcendentals=2 * rows * hidden,
        ),
    )(me, x, c, w_router, w_in, w_out)


def axis_bits(size):
    return [1 << b for b in range(size.bit_length() - 1)]


def exchange(value, axis, bit):
    size = lax.axis_size(axis)
    return lax.ppermute(value, axis, [(i, i ^ bit) for i in range(size)])


def gather_rows(block, axis):
    size = lax.axis_size(axis)
    me = lax.axis_index(axis)
    held = block[None]
    for bit in reversed(axis_bits(size)):
        got = exchange(held, axis, bit)
        upper = (me // bit) % 2
        both = jnp.where(upper == 0, jnp.stack([held, got]), jnp.stack([got, held]))
        held = jnp.moveaxis(both, 0, 1).reshape((-1,) + block.shape)
    return held.reshape((-1,) + block.shape[1:])


def scatter_rows(value, axis):
    size = lax.axis_size(axis)
    me = lax.axis_index(axis)
    held = value.reshape((size, value.shape[0] // size) + value.shape[1:])
    for bit in axis_bits(size):
        view = held.reshape((held.shape[0] // 2, 2) + held.shape[1:])
        mine = (me // bit) % 2
        away = lax.dynamic_index_in_dim(view, 1 - mine, 1, keepdims=False)
        keep = lax.dynamic_index_in_dim(view, mine, 1, keepdims=False)
        got = exchange(away.astype(BF), axis, bit)
        held = keep.astype(F32) + got.astype(F32)
    return held[0]


def sum_owners(value):
    owners = lax.axis_size("expert")
    rows, cols = value.shape
    parts = value.astype(BF).reshape(owners, rows // owners, cols)
    got = lax.all_to_all(parts, "expert", split_axis=0, concat_axis=0, tiled=True)
    total = jnp.sum(got.astype(F32), axis=0).astype(BF)
    spread = jnp.broadcast_to(total[None], got.shape)
    back = lax.all_to_all(spread, "expert", split_axis=0, concat_axis=0, tiled=True)
    return back.reshape(rows, cols).astype(F32)


def trade(rows):
    owners = lax.axis_size("expert")
    view = rows.reshape(owners, rows.shape[0] // owners, rows.shape[1])
    return lax.all_to_all(view, "expert", split_axis=0, concat_axis=0, tiled=True).reshape(rows.shape)


def body(
    tokens, routes, capacity, ln1_gain, ln1_bias, ln2_gain, ln2_bias,
    w_qkv, w_proj, w_router, w_in, w_out, cotangent,
):
    count, width = tokens.shape
    experts = capacity.shape[0]
    owners = lax.axis_size("expert")
    shards = lax.axis_size("shard")
    hidden = w_in.shape[2]
    images = count // SEQ
    padded = images * PAD_SEQ
    slot_count = 8 * ((2 * count + 8 * experts - 1) // (8 * experts))
    all_tokens = count * owners * shards
    me = lax.axis_index("expert").astype(jnp.int32).reshape(1)

    def pad_rows(values, fill=0):
        spread = values.reshape((images, SEQ) + values.shape[1:])
        room = [(0, 0), (0, PAD_SEQ - SEQ)] + [(0, 0)] * (values.ndim - 1)
        return jnp.pad(spread, room, constant_values=fill).reshape((padded,) + values.shape[1:])

    def cut_rows(values):
        spread = values.reshape((images, PAD_SEQ) + values.shape[1:])
        return spread[:, :SEQ].reshape((count,) + values.shape[1:])

    qkv_full = gather_rows(w_qkv, "shard")
    pack = jnp.concatenate([w_proj, jnp.pad(w_router, ((0, 0), (0, LANES - experts)))], axis=1)
    pack_full = gather_rows(pack, "shard")
    proj_full, router_full = pack_full[:, :width], pack_full[:, width:]

    labels = jnp.arange(experts, dtype=jnp.int32)[:, None]
    first, second = routes[:, 0][None, :], routes[:, 1][None, :]
    hit_first, hit_second = first == labels, second == labels
    hits = jnp.concatenate([hit_first, hit_second], axis=0).astype(BF)
    order = lax.broadcasted_iota(jnp.int32, (count, count), 0) < lax.broadcasted_iota(
        jnp.int32, (count, count), 1
    )
    before = dot_nn(hits, order.astype(BF))
    totals = jnp.sum(hits.astype(F32), axis=1, keepdims=True)
    before_first = before[:experts]
    before_second = before[experts:] + totals[:experts]
    limits = capacity[:, None].astype(F32)

    def slots(hit, ahead, choice):
        slot = jnp.sum(jnp.where(hit, ahead, 0.0), axis=0)
        limit = jnp.sum(jnp.where(hit, limits, 0.0), axis=0)
        kept = slot < limit
        slot = slot.astype(jnp.int32)
        return choice[0], slot, kept

    choices = [slots(hit_first, before_first, first), slots(hit_second, before_second, second)]
    head = 8 * ((slot_count + 15) // 16)
    sizes = (head, slot_count - head)

    def selector(chunk):
        size = sizes[chunk]
        at = lax.broadcasted_iota(jnp.int32, (experts * size, 1), 0)
        found = None
        for choice, slot, kept in choices:
            inside = slot - (0 if chunk == 0 else head)
            valid = kept & (inside >= 0) & (inside < size)
            where = pad_rows(jnp.where(valid, choice * size + inside, -1), -1)
            match = at == where[None, :]
            found = match if found is None else (found | match)
        return found.astype(BF)

    select = [selector(0), selector(1)]

    cot_pad = pad_rows(cotangent)
    cots = [trade(dot_nn(s, cot_pad).astype(BF)) for s in select]

    tok_pad = pad_rows(tokens)
    first_low, qkv_rows, heads_out = attend(tok_pad, ln1_gain, ln1_bias, qkv_full, images)
    token_rows = tok_pad.astype(F32)
    after_attention = token_rows + dot_nn(heads_out, proj_full)
    normed_two, inverse_two = norm_rows(after_attention)
    mid_low = (normed_two * ln2_gain + ln2_bias).astype(BF)

    mids = [trade(dot_nn(s, mid_low).astype(BF)) for s in select]
    done = [
        run_expert(me, mids[i], cots[i], router_full, w_in[0], w_out[0], experts) for i in range(2)
    ]
    backs = [trade(d[4]) for d in done]
    returned = [trade(d[3]) for d in done]
    grad_in_whole = dot_tn(mids[0], done[0][1]) + dot_tn(mids[1], done[1][1])
    grad_out_whole = dot_tn(done[0][0], done[0][2]) + dot_tn(done[1][0], done[1][2])
    grad_expert_in = lax.psum_scatter(
        grad_in_whole.astype(BF), "shard", scatter_dimension=1, tiled=True
    ).astype(F32)
    grad_expert_out = lax.psum_scatter(
        grad_out_whole.astype(BF), "shard", scatter_dimension=0, tiled=True
    ).astype(F32)

    logits = dot_nn(mid_low, router_full)[:, :experts]
    live = (lax.broadcasted_iota(jnp.int32, (padded, 1), 0) % PAD_SEQ) < SEQ
    gate_probs = jnp.where(live, jax.nn.softmax(logits, axis=-1), 0.0)
    counts = (totals[:experts] + totals[experts:])[:, 0]
    count_all, prob_all = lax.psum((counts, jnp.sum(gate_probs, axis=0)), ("expert", "shard"))
    route_share = count_all / (2.0 * all_tokens)
    balance_loss = experts * jnp.sum(route_share * prob_all / all_tokens)
    push = LOSS_WEIGHT * experts * route_share[None, :] / all_tokens
    grad_logits = gate_probs * (push - jnp.sum(gate_probs * push, axis=-1, keepdims=True))
    grad_logits = jnp.pad(grad_logits, ((0, 0), (0, LANES - experts))).astype(BF)
    grad_router = dot_tn(mid_low, grad_logits) + (done[0][5] + done[1][5]).T

    grad_mid = (
        dot_tn(select[0], backs[0]) + dot_tn(select[1], backs[1]) + dot_nt(grad_logits, router_full)
    )
    grad_gain_two = jnp.sum(grad_mid * normed_two, axis=0)
    grad_bias_two = jnp.sum(grad_mid, axis=0)
    grad_after = cot_pad.astype(F32) + norm_back(grad_mid, normed_two, inverse_two, ln2_gain)
    grad_heads = grad_after.astype(BF)
    grad_proj = dot_tn(heads_out, grad_heads)
    grad_heads_out = dot_nt(grad_heads, proj_full).astype(BF)

    mixed = cut_rows(
        after_attention + dot_tn(select[0], returned[0]) + dot_tn(select[1], returned[1])
    ).astype(BF)

    groups = 2
    cols = width // groups
    grad_first = None
    pieces = []
    for group in range(groups):
        grads = attend_back(qkv_rows, grad_heads_out, images, group, groups)
        for part in range(3):
            at = slice(part * width + group * cols, part * width + (group + 1) * cols)
            term = dot_nt(grads[part], qkv_full[:, at])
            grad_first = term if grad_first is None else grad_first + term
        pieces.append(jnp.concatenate([dot_tn(first_low, g) for g in grads], axis=1))
    normed_one, inverse_one = norm_rows(token_rows)
    grad_gain_one = jnp.sum(grad_first * normed_one, axis=0)
    grad_bias_one = jnp.sum(grad_first, axis=0)
    grad_tokens = cut_rows(grad_after + norm_back(grad_first, normed_one, inverse_one, ln1_gain))

    vectors = lax.psum(
        jnp.concatenate(
            [
                jnp.stack([grad_gain_one, grad_bias_one, grad_gain_two, grad_bias_two], axis=0),
                grad_router[:, :experts].T,
            ],
            axis=0,
        ),
        ("expert", "shard"),
    )
    own = width // shards
    vectors = lax.dynamic_slice_in_dim(vectors, lax.axis_index("shard") * own, own, axis=1)

    proj_total = sum_owners(scatter_rows(grad_proj, "shard"))
    totals_qkv = [sum_owners(scatter_rows(p, "shard")) for p in pieces]
    grad_qkv_weight = jnp.concatenate(
        [t[:, part * cols : (part + 1) * cols] for part in range(3) for t in totals_qkv], axis=1
    )
    return (
        mixed,
        balance_loss,
        grad_tokens,
        vectors[0],
        vectors[1],
        vectors[2],
        vectors[3],
        grad_qkv_weight,
        proj_total,
        vectors[4:].T,
        grad_expert_in[None],
        grad_expert_out[None],
    )


def solution(mesh):
    rows = P(("expert", "shard"), None)
    in_specs = (
        rows, rows, P(), P(), P(), P(), P(),
        P("shard", None), P("shard", None), P("shard", None),
        P("expert", None, None), P("expert", None, None), rows,
    )
    out_specs = (
        rows, P(), rows, P("shard"), P("shard"), P("shard"), P("shard"),
        P("shard", None), P("shard", None), P("shard", None),
        P("expert", None, "shard"), P("expert", "shard", None),
    )
    return jax.shard_map(body, mesh=mesh, in_specs=in_specs, out_specs=out_specs, check_vma=False)
```

time: 954 us -> 590 us (0.62)
  waiting for transfers between devices: 278 us -> 85.5 us
  matrix products: 227 us -> 99.3 us
  Pallas kernels: 0 us -> 120 us
  local copies, waits for them, and re-layouts: 154 us -> 48.6 us
  blocking collectives: 169 us -> 89.2 us
  starting transfers between devices: 18.6 us -> 75.1 us
  other arithmetic: 79 us -> 47.6 us
    dot_general x20 -> x31, matrix products: 226 us -> 99.3 us  [the longest x16 55.8 us: dot_tn(): lax.dot_general(left, right, (((0,), (0,)), ((), ())), preferred_element_...]
    pallas_call x0 -> x5, Pallas kernels: none -> 120 us  [the longest x2 86.8 us: run_expert(): pl.pallas_call(functools.partial(expert_kernel, experts=experts, block=bl...]
    psum x1 -> x0, waiting for transfers between devices: 113 us -> none  [body(): lax.psum((shares[0], shares[1], shares[2], shares[3], shares[4], shares[5...]
    reduce_scatter x4 -> x2, waiting for transfers between devices: 77.7 us -> 0.01 us  [the longest x1 0.01 us: body(): lax.psum_scatter(grad_in_whole.astype(BF), 'shard', scatter_dimension=1,...]
    psum x3 -> x2, blocking collectives: 151 us -> 89.2 us  [body(): lax.psum((counts, jnp.sum(gate_probs, axis=0)), ('expert', 'shard'))]
    all_to_all x4 -> x14, starting transfers between devices: 17.8 us -> 65.4 us  [the longest x8 41 us: trade(): lax.all_to_all(view, 'expert', split_axis=0, concat_axis=0, tiled=True)]
    gather x9 -> x0, local copies, waits for them, and re-layouts: 40.2 us -> none  [the longest x5 16.2 us: body(): gates = jnp.take_along_axis(gate_probs, routes, axis=1)]
    reduce_sum x8, other arithmetic: 27.8 us -> 1.66 us  [the longest x1 0.64 us: body(): jnp.sum(gate_probs * push, axis=-1, keepdims=True)]
  transfers between devices with their start and end apart: 12 -> 26, of which waited for: 6 -> 11; matrix products, arithmetic and copies ran while one was open for 35% -> 29% of each run, Pallas kernels for 0% -> 13%
where the time goes in v1:
time: 590 us; the launch traced here: 582 us
  Pallas kernels  120 us (20%)
  matrix products  99.3 us (17%)
  blocking collectives  89.2 us (15%)
  waiting for transfers between devices  85.5 us (14%)
  starting transfers between devices  75.1 us (13%)
  local copies, waits for them, and re-layouts  48.6 us (8%)
  other arithmetic  47.6 us (8%)
  between operations  17.1 us (3%)
    psum x2, blocking collectives, body(): lax.psum((counts, jnp.sum(gate_probs, axis=0)), ('expert', 'shard'))  89.2 us
    pallas_call x2, Pallas kernels, run_expert(): pl.pallas_call(functools.partial(expert_kernel, experts=experts, block=bl...  86.8 us
    dot_general x16, matrix products, dot_tn(): lax.dot_general(left, right, (((0,), (0,)), ((), ())), preferred_element_...  55.8 us
    all_to_all x8, starting transfers between devices, trade(): lax.all_to_all(view, 'expert', split_axis=0, concat_axis=0, tiled=True)  41 us
    all_to_all x8, waiting for transfers between devices, trade(): lax.all_to_all(view, 'expert', split_axis=0, concat_axis=0, tiled=True)  38.1 us
    dot_general x8, matrix products, dot_nt(): lax.dot_general(left, right, (((1,), (1,)), ((), ())), preferred_element_...  26.8 us
    pallas_call x2, Pallas kernels, attend_back(): pl.pallas_call(functools.partial(attend_back_kernel, scale=1.0 / math.sqr...  19.7 us
    all_to_all x3, waiting for transfers between devices, sum_owners(): lax.all_to_all(spread, 'expert', split_axis=0, concat_axis=0, tiled=True)  17.7 us
  transfers between devices with their start and end apart: 26, of which 11 were waited for; matrix products, arithmetic and copies ran while one was open for 29% of the time, Pallas kernels for 13%

profile of v1, /device:TPU:0, one launch (start us, length us, event | category | flops | bytes accessed | tf_op | source)
XLA Modules:
  0.0 582.1 jit_solution(10094718536199960611)
XLA Ops:
  7.2 3.0 collective-permute-start
  14.9 2.6 convolution_convert_fusion.3
  17.5 5.9 %all-to-all-start.4 = ((bf16[8,96,768]{2,1,0:T(8,128)(2,1)}), bf16[8,96,768]{2,1,0:T(8,128)(2,1)}, u32[]{:S(2)}, u32[]{:S(2)}) async-start(bf16[8,96,768]{2,1,0:T(8,128)(2,1)} %bitcast.158), calls=%async_computation.4 | async-start | bytes 2359296 | tf_op jit(solution)/shard_map/all_to_all | solution.py:328
  23.5 6.6 %collective-permute-done = bf16[1,192,2304]{2,1,0:T(8,128)(2,1)S(1)} collective-permute-done((bf16[1,192,2304]{2,1,0:T(8,128)(2,1)}, bf16[1,192,2304]{2,1,0:T(8,128)(2,1)S(1)}, u32[]{:S(2)}, u32[]{:S(2)}) %collective-permute-start) | collective-permute-done | bytes 884768 | tf_op jit(solution)/shard_map/ppermute | solution.py:285
  35.4 8.9 %collective-permute-done.2 = bf16[1,192,896]{2,1,0:T(8,128)(2,1)} collective-permute-done((bf16[1,192,896]{2,1,0:T(8,128)(2,1)}, bf16[1,192,896]{2,1,0:T(8,128)(2,1)}, u32[]{:S(2)}, u32[]{:S(2)}) %collective-permute-start.2) | collective-permute-done | bytes 344096 | tf_op jit(solution)/shard_map/ppermute | solution.py:285
  44.2 2.4 maximum_select_fusion.5
  46.6 2.8 convolution_convert_fusion.1
  59.0 6.2 %all-to-all-start.1 = ((bf16[8,104,768]{2,1,0:T(8,128)(2,1)}), bf16[8,104,768]{2,1,0:T(8,128)(2,1)}, u32[]{:S(2)}, u32[]{:S(2)}) async-start(bf16[8,104,768]{2,1,0:T(8,128)(2,1)} %bitcast.154), calls=%async_computation.1 | async-start | bytes 2555904 | tf_op jit(solution)/shard_map/all_to_all | solution.py:328
  65.3 2.5 fusion
  69.9 13.3 %shard_map.220 = (bf16[832,768]{1,0:T(8,128)(2,1)}, bf16[832,2304]{1,0:T(8,128)(2,1)}, bf16[832,768]{1,0:T(8,128)(2,1)}) custom-call(bf16[832,768]{1,0:T(8,128)(2,1)} %bitcast.123, f32[1,768]{1,0:T(1,128)} %reshape.439.gain_ref, f32[1,768]{1,0:T(1,128)} %reshape.440.bias_ref, bf16[768,2304]{1,0:T(8,128)(2,1)} %bitcast.126), custom_call_target="tpu_custom_call" | custom-call | flops 3476029440 | bytes 11206656 | tf_op jit(solution)/shard_map/pallas_call | solution.py:88
  83.1 2.6 fusion.70
  88.0 2.6 convolution_convert_fusion.4
  90.6 6.1 %all-to-all-done.1 = bf16[8,104,768]{2,1,0:T(8,128)(2,1)} async-done(((bf16[8,104,768]{2,1,0:T(8,128)(2,1)}), bf16[8,104,768]{2,1,0:T(8,128)(2,1)}, u32[]{:S(2)}, u32[]{:S(2)}) %all-to-all-start.1) | async-done | bytes 1277984 | tf_op jit(solution)/shard_map/all_to_all | solution.py:328
  96.7 4.3 all-to-all-start.3
  100.9 4.1 convolution_convert_fusion.2
  105.0 24.3 %all-to-all-done.3 = bf16[8,96,768]{2,1,0:T(8,128)(2,1)} async-done(((bf16[8,96,768]{2,1,0:T(8,128)(2,1)}), bf16[8,96,768]{2,1,0:T(8,128)(2,1)}, u32[]{:S(2)}, u32[]{:S(2)}) %all-to-all-start.3) | async-done | bytes 1179680 | tf_op jit(solution)/shard_map/all_to_all | solution.py:328
  129.3 4.3 all-to-all-start
  135.5 42.5 %shard_map.222 = (bf16[768,3072]{1,0:T(8,128)(2,1)}, bf16[768,3072]{1,0:T(8,128)(2,1)}, bf16[768,768]{1,0:T(8,128)(2,1)}, bf16[768,768]{1,0:T(8,128)(2,1)}, bf16...) custom-call(s32[1]{0:T(128)} %bitcast.13.me_ref, bf16[768,768]{1,0:T(8,128)(2,1)} %bitcast.24.x_ref, ...), custom_call_target="tpu_custom_call" | custom-call | flops 14495514624 | bytes 25952256 | tf_op jit(solution)/shard_map/pallas_call | solution.py:245
  178.0 44.2 %shard_map.221 = (bf16[832,3072]{1,0:T(8,128)(2,1)}, bf16[832,3072]{1,0:T(8,128)(2,1)}, bf16[832,768]{1,0:T(8,128)(2,1)}, bf16[832,768]{1,0:T(8,128)(2,1)}, bf16...) custom-call(s32[1]{0:T(128)} %bitcast.13.me_ref, bf16[832,768]{1,0:T(8,128)(2,1)} %bitcast.15.x_ref, ...), custom_call_target="tpu_custom_call" | custom-call | flops 15703474176 | bytes 27328512 | tf_op jit(solution)/shard_map/pallas_call | solution.py:245
  222.3 7.6 %fusion.78 = f32[768,3072]{1,0:T(8,128)S(1)} fusion(bf16[832,768]{1,0:T(8,128)(2,1)} %bitcast.15.x_ref, bf16[832,3072]{1,0:T(8,128)(2,1)} %get-tuple-element.48), kind=kOutput, calls=%fused_computation.168 | convolution fusion | flops 3925868544 | bytes 15826944 | tf_op jit(solution)/shard_map/dot_general | solution.py:33
  229.8 7.4 %add_convert_fusion.1 = bf16[768,3072]{1,0:T(8,128)(2,1)} fusion(f32[768,3072]{1,0:T(8,128)S(1)} %fusion.78, bf16[768,768]{1,0:T(8,128)(2,1)} %bitcast.24.x_ref, bf16[768,3072]{1,0:T(8,128)(2,1)S(1)} %copy-done.37), kind=kOutput, calls=%fused_computation.1 | convolution fusion | flops 3628597248 | bytes 20054016 | tf_op jit(solution)/shard_map/dot_general | solution.py:33
  237.2 5.9 %all-to-all-start.7 = ((bf16[8,96,768]{2,1,0:T(8,128)(2,1)}), bf16[8,96,768]{2,1,0:T(8,128)(2,1)}, u32[]{:S(2)}, u32[]{:S(2)}) async-start(bf16[8,96,768]{2,1,0:T(8,128)(2,1)} %bitcast.159), calls=%async_computation.7 | async-start | bytes 2359296 | tf_op jit(solution)/shard_map/all_to_all | solution.py:328
  243.1 47.9 %psum.21 = f32[8]{0:T(128)S(1)} all-reduce(f32[8]{0:T(128)S(1)} %get-tuple-element.86), channel_id=1, replica_groups=mesh['expert'=8,'shard'=4] {'expert','shard'}, use_global_device_ids=true, to_apply=%region_7.8 | all-reduce | flops 8 | bytes 64 | tf_op jit(solution)/shard_map/psum | solution.py:427
  298.7 5.5 all-to-all-start.6
  304.2 7.5 %fusion.79 = f32[3072,768]{1,0:T(8,128)S(1)} fusion(bf16[832,3072]{1,0:T(8,128)(2,1)} %get-tuple-element.50, bf16[832,768]{1,0:T(8,128)(2,1)} %get-tuple-element.51), kind=kOutput, calls=%fused_computation.169 | convolution fusion | flops 3925868544 | bytes 15826944 | tf_op jit(solution)/shard_map/dot_general | solution.py:33
  311.8 8.2 %add_convert_fusion = bf16[3072,768]{1,0:T(8,128)(2,1)} fusion(f32[3072,768]{1,0:T(8,128)S(1)} %fusion.79, bf16[768,3072]{1,0:T(8,128)(2,1)} %get-tuple-element.52, bf16[768,768]{1,0:T(8,128)(2,1)S(1)} %copy-done.38), kind=kOutput, calls=%fused_computation | convolution fusion | flops 3628597248 | bytes 20054016 | tf_op jit(solution)/shard_map/dot_general | solution.py:33
  322.1 4.0 fusion.24
  326.1 7.7 %all-to-all-done.6 = bf16[8,104,768]{2,1,0:T(8,128)(2,1)} async-done(((bf16[8,104,768]{2,1,0:T(8,128)(2,1)}), bf16[8,104,768]{2,1,0:T(8,128)(2,1)}, u32[]{:S(2)}, u32[]{:S(2)}) %all-to-all-start.6) | async-done | bytes 1277984 | tf_op jit(solution)/shard_map/all_to_all | solution.py:328
  333.8 4.4 all-to-all-start.5
  338.3 3.4 fusion.16
  346.8 2.9 fusion.32
  349.7 9.7 %shard_map.224 = (bf16[832,384]{1,0:T(8,128)(2,1)}, bf16[832,384]{1,0:T(8,128)(2,1)}, bf16[832,384]{1,0:T(8,128)(2,1)}) custom-call(bf16[832,2304]{1,0:T(8,128)(2,1)} %get-tuple-element.38.q_ref.k_ref.v_ref, bf16[832,2304]{1,0:T(8,128)(2,1)} %get-tuple-element.38.q_ref.k_ref.v_ref, bf16[832,2304]{1,0:T(8,128)(2,1)} %get-tuple-element.38.q_ref.k_ref.v_ref, ...), custom_call_target="tpu_custom_call" | custom-call | flops 664535040 | bytes 4472832 | tf_op jit(solution)/shard_map/pallas_call | solution.py:156
  359.4 10.0 %shard_map.223 = (bf16[832,384]{1,0:T(8,128)(2,1)}, bf16[832,384]{1,0:T(8,128)(2,1)}, bf16[832,384]{1,0:T(8,128)(2,1)}) custom-call(bf16[832,2304]{1,0:T(8,128)(2,1)} %get-tuple-element.38.q_ref.k_ref.v_ref, bf16[832,2304]{1,0:T(8,128)(2,1)} %get-tuple-element.38.q_ref.k_ref.v_ref, bf16[832,2304]{1,0:T(8,128)(2,1)} %get-tuple-element.38.q_ref.k_ref.v_ref, ...), custom_call_target="tpu_custom_call" | custom-call | flops 664535040 | bytes 4472832 | tf_op jit(solution)/shard_map/pallas_call | solution.py:156
  371.0 3.4 fusion.45
  378.7 2.3 fusion.41
  381.1 2.3 fusion.43
  392.3 2.3 fusion.37
  394.6 5.2 copy.31
  399.8 2.5 fusion.29
  402.3 5.2 copy.32
  409.6 6.0 %all-to-all-start.12 = ((bf16[8,24,768]{2,1,0:T(8,128)(2,1)}), bf16[8,24,768]{2,1,0:T(8,128)(2,1)S(1)}, u32[]{:S(2)}, u32[]{:S(2)}) async-start(bf16[8,24,768]{2,1,0:T(8,128)(2,1)} %bitcast.56), calls=%async_computation.12 | async-start | bytes 589824 | tf_op jit(solution)/shard_map/all_to_all | solution.py:318
  415.6 3.6 fusion.39
  419.1 2.5 fusion.30
  421.7 3.9 all-to-all-done.12
  425.6 4.5 all-to-all-start.2
  430.1 8.9 %fusion.12 = (f32[768]{0:T(1024)S(1)}, f32[832]{0:T(1024)S(1)}, f32[832]{0:T(1024)S(1)}, f32[768]{0:T(1024)S(1)}, f32[832,768]{1,0:T(8,128)}) fusion(f32[832]{0:T(1024)S(1)} %div.78, f32[832]{0:T(1024)S(1)} %rsqrt.21, bf16[4,208,768]{2,1,0:T(8,128)(2,1)} %pad.29, bf16[832,768]{1,0:T(8,128)(2,1)} %bitcast.124, f32[768]{0:T(1024)S(1)} %copy-done.27, ...), kind=kOutput, calls=%fused_computation.26 | convolution fusion | flops 502231936 | bytes 19142656 | tf_op jit(solution)/shard_map/dot_general | solution.py:29
  439.2 41.3 %all-reduce.8 = (f32[8]{0:T(128)S(1)}, f32[12,768]{1,0:T(8,128)S(1)}) all-reduce(f32[8]{0:T(128)} %get-tuple-element.65, f32[12,768]{1,0:T(8,128)S(1)} %concatenate.60), channel_id=1, replica_groups=mesh['expert'=8,'shard'=4] {'expert','shard'}, use_global_device_ids=true, to_apply=%region_11.12 | all-reduce | flops 9224 | bytes 73792 | tf_op jit(solution)/shard_map/psum | solution.py:427
  483.9 2.3 collective-permute-start.5
  486.2 2.6 bitcast_add_fusion
  489.6 3.9 all-to-all-start.13
  498.3 3.6 all-to-all-done.13
  502.0 3.5 all-to-all-start.8
  505.5 4.8 fusion.18
  512.1 3.6 all-to-all-done.8
  515.8 3.7 all-to-all-start.10
  519.4 3.4 add_convert_fusion.2
  524.4 6.7 %all-to-all-done.10 = bf16[8,24,1152]{2,1,0:T(8,128)(2,1)S(1)} async-done(((bf16[8,24,1152]{2,1,0:T(8,128)(2,1)}), bf16[8,24,1152]{2,1,0:T(8,128)(2,1)S(1)}, u32[]{:S(2)}, u32[]{:S(2)}) %all-to-all-start.10) | async-done | bytes 442400 | tf_op jit(solution)/shard_map/all_to_all | solution.py:318
  531.9 3.7 all-to-all-start.9
  535.6 3.0 fusion.11
  543.1 4.5 all-to-all-done.9
  548.5 3.6 all-to-all-start.11
  554.8 9.5 %all-to-all-done.11 = bf16[8,24,1152]{2,1,0:T(8,128)(2,1)S(1)} async-done(((bf16[8,24,1152]{2,1,0:T(8,128)(2,1)}), bf16[8,24,1152]{2,1,0:T(8,128)(2,1)S(1)}, u32[]{:S(2)}, u32[]{:S(2)}) %all-to-all-start.11) | async-done | bytes 442400 | tf_op jit(solution)/shard_map/all_to_all | solution.py:321
  568.0 2.8 bitcast_convert_fusion.1
  570.9 2.8 bitcast_convert_fusion
  (219 shorter events, 81.8 us)
Async XLA Ops:
  7.2 22.9 %collective-permute-start = (bf16[1,192,2304]{2,1,0:T(8,128)(2,1)}, bf16[1,192,2304]{2,1,0:T(8,128)(2,1)S(1)}, u32[]{:S(2)}, u32[]{:S(2)}) collective-permute-start(bf16[1,192,2304]{2,1,0:T(8,128)(2,1)} %bitcast.140), channel_id=1, source_target_pairs={{0,2},{1,3},{2,0},{3,1},{4,6},{5,7},{6,4},{7,5},{8,10},{9,11},{10,... | collective-permute-start | bytes 2654216 | tf_op jit(solution)/shard_map/ppermute | solution.py:285
  14.9 31.7 %copy-start.10 = (bf16[4,208,768]{2,1,0:T(8,128)(2,1)}, bf16[4,208,768]{2,1,0:T(8,128)(2,1)S(1)}, u32[]{:S(2)}) copy-start(bf16[4,208,768]{2,1,0:T(8,128)(2,1)S(1)} %pad.33) | copy-start | bytes 3833860
  17.5 12.6 %copy-start.13 = (bf16[192,2304]{1,0:T(8,128)(2,1)S(1)}, bf16[192,2304]{1,0:T(8,128)(2,1)}, u32[]{:S(2)}) copy-start(bf16[192,2304]{1,0:T(8,128)(2,1)} %param.20) | copy-start | bytes 2654212
  17.5 14.0 %copy-start.31 = (bf16[192,8]{0,1:T(8,128)(2,1)S(1)}, bf16[192,8]{0,1:T(8,128)(2,1)}, u32[]{:S(2)}) copy-start(bf16[192,8]{0,1:T(8,128)(2,1)} %param.22) | copy-start | bytes 9220
  17.5 41.5 %all-to-all-start.4 = ((bf16[8,96,768]{2,1,0:T(8,128)(2,1)}), bf16[8,96,768]{2,1,0:T(8,128)(2,1)}, u32[]{:S(2)}, u32[]{:S(2)}) async-start(bf16[8,96,768]{2,1,0:T(8,128)(2,1)} %bitcast.158), calls=%async_computation.4 | async-start | bytes 2359296 | tf_op jit(solution)/shard_map/all_to_all | solution.py:328
  31.6 33.7 %collective-permute-start.1 = (bf16[2,192,2304]{2,1,0:T(8,128)(2,1)}, bf16[2,192,2304]{2,1,0:T(8,128)(2,1)}, u32[]{:S(2)}, u32[]{:S(2)}) collective-permute-start(bf16[2,192,2304]{2,1,0:T(8,128)(2,1)} %maximum_select_fusion.2), channel_id=1, source_target_pairs={{0,1},{1,0},{2,3},{3,2},{4,5},{5,4},{6,7},{7,6},{8,9},{9,8},{10,11... | collective-permute-start | bytes 5308424 | tf_op jit(solution)/shard_map/ppermute | solution.py:285
  33.4 10.8 %collective-permute-start.2 = (bf16[1,192,896]{2,1,0:T(8,128)(2,1)}, bf16[1,192,896]{2,1,0:T(8,128)(2,1)}, u32[]{:S(2)}, u32[]{:S(2)}) collective-permute-start(bf16[1,192,896]{2,1,0:T(8,128)(2,1)} %get-tuple-element.77), channel_id=1, source_target_pairs={{0,2},{1,3},{2,0},{3,1},{4,6},{5,7},{6,4},{7,5},{8,10},{9,11},{10,... | collective-permute-start | bytes 1032200 | tf_op jit(solution)/shard_map/ppermute | solution.py:285
  35.4 302.9 %copy-start.29 = (s32[832]{0:T(1024)}, s32[832]{0:T(1024)S(1)}, u32[]{:S(2)}) copy-start(s32[832]{0:T(1024)S(1)} %eq.122) | copy-start | bytes 9988
  46.6 2.8 copy-start.28
  46.6 3.4 copy-start.27
  46.6 9.5 %collective-permute-start.3 = (bf16[2,192,896]{2,1,0:T(8,128)(2,1)}, bf16[2,192,896]{2,1,0:T(8,128)(2,1)}, u32[]{:S(2)}, u32[]{:S(2)}) collective-permute-start(bf16[2,192,896]{2,1,0:T(8,128)(2,1)} %maximum_select_fusion.5), channel_id=1, source_target_pairs={{0,1},{1,0},{2,3},{3,2},{4,5},{5,4},{6,7},{7,6},{8,9},{9,8},{10,11... | collective-permute-start | bytes 2064392 | tf_op jit(solution)/shard_map/ppermute | solution.py:285
  52.2 4.0 copy-start.2
  57.8 7.5 %copy-start.7 = (bf16[1,2,192,2304]{3,2,1,0:T(8,128)(2,1)S(1)}, bf16[1,2,192,2304]{3,2,1,0:T(8,128)(2,1)}, u32[]{:S(2)}) copy-start(bf16[1,2,192,2304]{3,2,1,0:T(8,128)(2,1)} %maximum_select_fusion.1) | copy-start | bytes 5308420
  59.0 37.6 %all-to-all-start.1 = ((bf16[8,104,768]{2,1,0:T(8,128)(2,1)}), bf16[8,104,768]{2,1,0:T(8,128)(2,1)}, u32[]{:S(2)}, u32[]{:S(2)}) async-start(bf16[8,104,768]{2,1,0:T(8,128)(2,1)} %bitcast.154), calls=%async_computation.1 | async-start | bytes 2555904 | tf_op jit(solution)/shard_map/all_to_all | solution.py:328
  69.9 13.3 %copy-start = (bf16[4,208,768]{2,1,0:T(8,128)(2,1)S(1)}, bf16[4,208,768]{2,1,0:T(8,128)(2,1)}, u32[]{:S(2)}) copy-start(bf16[4,208,768]{2,1,0:T(8,128)(2,1)} %pad.29) | copy-start | bytes 3833860
  69.9 13.3 %copy-start.14 = (bf16[2,2,192,896]{3,2,1,0:T(8,128)(2,1)S(1)}, bf16[2,2,192,896]{3,2,1,0:T(8,128)(2,1)}, u32[]{:S(2)}) copy-start(bf16[2,2,192,896]{3,2,1,0:T(8,128)(2,1)} %copy.30) | copy-start | bytes 4128772
  85.7 0.7 copy-start.32
  86.9 1.1 copy-start.4
  96.7 32.7 %all-to-all-start.3 = ((bf16[8,96,768]{2,1,0:T(8,128)(2,1)}), bf16[8,96,768]{2,1,0:T(8,128)(2,1)}, u32[]{:S(2)}, u32[]{:S(2)}) async-start(bf16[8,96,768]{2,1,0:T(8,128)(2,1)} %bitcast.160), calls=%async_computation.3 | async-start | bytes 2359296 | tf_op jit(solution)/shard_map/all_to_all | solution.py:328
  129.3 48.7 %all-to-all-start = ((bf16[8,104,768]{2,1,0:T(8,128)(2,1)}), bf16[8,104,768]{2,1,0:T(8,128)(2,1)}, u32[]{:S(2)}, u32[]{:S(2)}) async-start(bf16[8,104,768]{2,1,0:T(8,128)(2,1)} %bitcast.155), calls=%async_computation | async-start | bytes 2555904 | tf_op jit(solution)/shard_map/all_to_all | solution.py:328
  133.6 434.4 %reduce-scatter.3.cloned.1.call-start = ((), (), s32[]{:S(2)}) async-start(), calls=%async_computation.16 | async-start | bytes 5898240 | tf_op jit(solution)/shard_map/reduce_scatter | solution.py:416
  222.3 7.6 %copy-start.37 = (bf16[768,3072]{1,0:T(8,128)(2,1)S(1)}, bf16[768,3072]{1,0:T(8,128)(2,1)}, u32[]{:S(2)}) copy-start(bf16[768,3072]{1,0:T(8,128)(2,1)} %get-tuple-element.49) | copy-start | bytes 14155780
  237.2 61.5 %all-to-all-start.7 = ((bf16[8,96,768]{2,1,0:T(8,128)(2,1)}), bf16[8,96,768]{2,1,0:T(8,128)(2,1)}, u32[]{:S(2)}, u32[]{:S(2)}) async-start(bf16[8,96,768]{2,1,0:T(8,128)(2,1)} %bitcast.159), calls=%async_computation.7 | async-start | bytes 2359296 | tf_op jit(solution)/shard_map/all_to_all | solution.py:328
  291.0 7.7 %copy-start.33 = (f32[8]{0:T(128)}, f32[8]{0:T(128)S(1)}, u32[]{:S(2)}) copy-start(f32[8]{0:T(128)S(1)} %psum.21) | copy-start | bytes 100
  298.7 35.1 %all-to-all-start.6 = ((bf16[8,104,768]{2,1,0:T(8,128)(2,1)}), bf16[8,104,768]{2,1,0:T(8,128)(2,1)}, u32[]{:S(2)}, u32[]{:S(2)}) async-start(bf16[8,104,768]{2,1,0:T(8,128)(2,1)} %bitcast.153), calls=%async_computation.6 | async-start | bytes 2555904 | tf_op jit(solution)/shard_map/all_to_all | solution.py:328
  304.2 266.7 %reduce-scatter.5.cloned.1.call-start = ((), (), s32[]{:S(2)}) async-start(), calls=%async_computation.17 | async-start | bytes 5898240 | tf_op jit(solution)/shard_map/reduce_scatter | solution.py:419
  304.2 7.6 %copy-start.38 = (bf16[768,768]{1,0:T(8,128)(2,1)S(1)}, bf16[768,768]{1,0:T(8,128)(2,1)}, u32[]{:S(2)}) copy-start(bf16[768,768]{1,0:T(8,128)(2,1)} %get-tuple-element.53) | copy-start | bytes 3538948
  320.0 1.0 copy-start.25
  333.8 75.8 %all-to-all-start.5 = ((bf16[8,96,768]{2,1,0:T(8,128)(2,1)}), bf16[8,96,768]{2,1,0:T(8,128)(2,1)}, u32[]{:S(2)}, u32[]{:S(2)}) async-start(bf16[8,96,768]{2,1,0:T(8,128)(2,1)} %bitcast.157), calls=%async_computation.5 | async-start | bytes 2359296 | tf_op jit(solution)/shard_map/all_to_all | solution.py:328
  338.3 3.4 copy-start.15
  338.3 3.4 copy-start.16
  341.7 1.7 copy-start.11
  344.5 2.3 copy-start.6
  344.5 2.3 copy-start.36
  359.4 11.6 %copy-start.3 = (bf16[2,2,192,2304]{3,2,1,0:T(8,128)(2,1)S(1)}, bf16[2,2,192,2304]{3,2,1,0:T(8,128)(2,1)}, u32[]{:S(2)}) copy-start(bf16[2,2,192,2304]{3,2,1,0:T(8,128)(2,1)} %copy.28) | copy-start | bytes 10616836
  369.4 5.0 copy-start.24
  369.4 5.0 copy-start.35
  370.9 18.2 %collective-permute-start.8 = (bf16[2,192,768]{2,1,0:T(8,128)(2,1)S(1)}, bf16[2,192,768]{2,1,0:T(8,128)(2,1)S(1)}, u32[]{:S(2)}, u32[]{:S(2)}) collective-permute-start(bf16[2,192,768]{2,1,0:T(8,128)(2,1)S(1)} %fusion.35), channel_id=1, source_target_pairs={{0,1},{1,0},{2,3},{3,2},{4,5},{5,4},{6,7},{7,6},{8,9},{9,8},{10,11... | collective-permute-start | bytes 1769480 | tf_op jit(solution)/shard_map/ppermute | solution.py:285
  374.4 1.1 copy-start.20
  375.5 1.1 copy-start.21
  376.6 1.1 copy-start.19
  377.7 1.1 copy-start.22
  378.5 2.6 copy-start.23
  387.0 2.8 copy-start.17
  389.9 1.0 copy-start.12
  391.0 16.7 %collective-permute-start.9 = (bf16[1,192,768]{2,1,0:T(8,128)(2,1)S(1)}, bf16[1,192,768]{2,1,0:T(8,128)(2,1)}, u32[]{:S(2)}, u32[]{:S(2)}) collective-permute-start(bf16[1,192,768]{2,1,0:T(8,128)(2,1)S(1)} %dynamic-slice_convert_fusion.5), channel_id=1, source_target_pairs={{0,2},{1,3},{2,0},{3,1},{4,6},{5,7},{6,4},{7,5},{8,10},{9,11},{10,... | collective-permute-start | bytes 884744 | tf_op jit(solution)/shard_map/ppermute | solution.py:285
  407.5 73.1 %collective-permute-start.4 = (bf16[2,192,1152]{2,1,0:T(8,128)(2,1)}, bf16[2,192,1152]{2,1,0:T(8,128)(2,1)}, u32[]{:S(2)}, u32[]{:S(2)}) collective-permute-start(bf16[2,192,1152]{2,1,0:T(8,128)(2,1)} %fusion.29), channel_id=1, source_target_pairs={{0,1},{1,0},{2,3},{3,2},{4,5},{5,4},{6,7},{7,6},{8,9},{9,8},{10,11... | collective-permute-start | bytes 2654216 | tf_op jit(solution)/shard_map/ppermute | solution.py:285
  409.6 16.0 %all-to-all-start.12 = ((bf16[8,24,768]{2,1,0:T(8,128)(2,1)}), bf16[8,24,768]{2,1,0:T(8,128)(2,1)S(1)}, u32[]{:S(2)}, u32[]{:S(2)}) async-start(bf16[8,24,768]{2,1,0:T(8,128)(2,1)} %bitcast.56), calls=%async_computation.12 | async-start | bytes 589824 | tf_op jit(solution)/shard_map/all_to_all | solution.py:318
  421.6 64.6 %collective-permute-start.6 = (bf16[2,192,1152]{2,1,0:T(8,128)(2,1)}, bf16[2,192,1152]{2,1,0:T(8,128)(2,1)}, u32[]{:S(2)}, u32[]{:S(2)}) collective-permute-start(bf16[2,192,1152]{2,1,0:T(8,128)(2,1)} %fusion.30), channel_id=1, source_target_pairs={{0,1},{1,0},{2,3},{3,2},{4,5},{5,4},{6,7},{7,6},{8,9},{9,8},{10,11... | collective-permute-start | bytes 2654216 | tf_op jit(solution)/shard_map/ppermute | solution.py:285
  425.6 63.2 %all-to-all-start.2 = ((bf16[8,104,768]{2,1,0:T(8,128)(2,1)}), bf16[8,104,768]{2,1,0:T(8,128)(2,1)}, u32[]{:S(2)}, u32[]{:S(2)}) async-start(bf16[8,104,768]{2,1,0:T(8,128)(2,1)} %bitcast.152), calls=%async_computation.2 | async-start | bytes 2555904 | tf_op jit(solution)/shard_map/all_to_all | solution.py:328
  480.5 5.7 copy-start.5
  482.6 1.2 copy-start.9
  483.9 12.3 %collective-permute-start.5 = (bf16[1,192,1152]{2,1,0:T(8,128)(2,1)S(1)}, bf16[1,192,1152]{2,1,0:T(8,128)(2,1)}, u32[]{:S(2)}, u32[]{:S(2)}) collective-permute-start(bf16[1,192,1152]{2,1,0:T(8,128)(2,1)S(1)} %dynamic-slice_convert_fusion.4), channel_id=1, source_target_pairs={{0,2},{1,3},{2,0},{3,1},{4,6},{5,7},{6,4},{7,5},{8,10},{9,11},{10,... | collective-permute-start | bytes 1327112 | tf_op jit(solution)/shard_map/ppermute | solution.py:285
  488.8 16.7 %copy-start.30 = (s32[832]{0:T(1024)S(1)}, s32[832]{0:T(1024)}, u32[]{:S(2)}) copy-start(s32[832]{0:T(1024)} %copy-done.29) | copy-start | bytes 9988
  489.6 12.4 %all-to-all-start.13 = ((bf16[8,24,768]{2,1,0:T(8,128)(2,1)}), bf16[8,24,768]{2,1,0:T(8,128)(2,1)S(1)}, u32[]{:S(2)}, u32[]{:S(2)}) async-start(bf16[8,24,768]{2,1,0:T(8,128)(2,1)} %broadcast_in_dim.102), calls=%async_computation.13 | async-start | bytes 589824 | tf_op jit(solution)/shard_map/all_to_all | solution.py:321
  495.5 14.8 %collective-permute-start.7 = (bf16[1,192,1152]{2,1,0:T(8,128)(2,1)}, bf16[1,192,1152]{2,1,0:T(8,128)(2,1)}, u32[]{:S(2)}, u32[]{:S(2)}) collective-permute-start(bf16[1,192,1152]{2,1,0:T(8,128)(2,1)} %dynamic-slice_convert_fusion.3), channel_id=1, source_target_pairs={{0,2},{1,3},{2,0},{3,1},{4,6},{5,7},{6,4},{7,5},{8,10},{9,11},{10,... | collective-permute-start | bytes 1327112 | tf_op jit(solution)/shard_map/ppermute | solution.py:285
  502.0 8.3 %copy-start.18 = (bf16[8,24,768]{2,1,0:T(8,128)(2,1)}, bf16[8,24,768]{2,1,0:T(8,128)(2,1)S(1)}, u32[]{:S(2)}) copy-start(bf16[8,24,768]{2,1,0:T(8,128)(2,1)S(1)} %all-to-all-done.13) | copy-start | bytes 884740
  502.0 13.8 %all-to-all-start.8 = ((bf16[8,24,1152]{2,1,0:T(8,128)(2,1)}), bf16[8,24,1152]{2,1,0:T(8,128)(2,1)S(1)}, u32[]{:S(2)}, u32[]{:S(2)}) async-start(bf16[8,24,1152]{2,1,0:T(8,128)(2,1)} %bitcast.44), calls=%async_computation.8 | async-start | bytes 884736 | tf_op jit(solution)/shard_map/all_to_all | solution.py:318
  505.4 4.8 copy-start.8
  515.8 15.3 %all-to-all-start.10 = ((bf16[8,24,1152]{2,1,0:T(8,128)(2,1)}), bf16[8,24,1152]{2,1,0:T(8,128)(2,1)S(1)}, u32[]{:S(2)}, u32[]{:S(2)}) async-start(bf16[8,24,1152]{2,1,0:T(8,128)(2,1)} %bitcast.149), calls=%async_computation.10 | async-start | bytes 884736 | tf_op jit(solution)/shard_map/all_to_all | solution.py:318
  523.0 12.6 %copy-start.1 = (bf16[4,208,768]{2,1,0:T(8,128)(2,1)S(1)}, bf16[4,208,768]{2,1,0:T(8,128)(2,1)}, u32[]{:S(2)}) copy-start(bf16[4,208,768]{2,1,0:T(8,128)(2,1)} %pad.29) | copy-start | bytes 3833860
  531.9 15.8 %all-to-all-start.9 = ((bf16[8,24,1152]{2,1,0:T(8,128)(2,1)}), bf16[8,24,1152]{2,1,0:T(8,128)(2,1)S(1)}, u32[]{:S(2)}, u32[]{:S(2)}) async-start(bf16[8,24,1152]{2,1,0:T(8,128)(2,1)} %broadcast_in_dim.100), calls=%async_computation.9 | async-start | bytes 884736 | tf_op jit(solution)/shard_map/all_to_all | solution.py:321
  538.8 1.7 copy-start.34
  548.5 15.8 %all-to-all-start.11 = ((bf16[8,24,1152]{2,1,0:T(8,128)(2,1)}), bf16[8,24,1152]{2,1,0:T(8,128)(2,1)S(1)}, u32[]{:S(2)}, u32[]{:S(2)}) async-start(bf16[8,24,1152]{2,1,0:T(8,128)(2,1)} %broadcast_in_dim.101), calls=%async_computation.11 | async-start | bytes 884736 | tf_op jit(solution)/shard_map/all_to_all | solution.py:321
  (1 other events, 0.7 us)
Sparse Core Ops, SparseCore 0:
  237.3 49.3 reduce-scatter.2
  320.2 48.6 reduce-scatter.4
